TPU v7x, 32 devices: a whole 2x2x4 slice. The times are simulated.
32 devices in a mesh: row: 4 (over y, core), col: 8 (over z, x).
Axes of the slice: x: 2, y: 2, z: 4, core: 2. Of those that a mesh axis runs over, the one named last changes fastest.
Arguments:
- covariance: float32 [9216, 9216], P('row', 'col'), may hold values from -1 to 10, as said below
- samples: float32 [192, 9216], P(None, ('col', 'row')), may hold values from -2 to 2
- labels: int32 [192], replicated, may hold values from 0 to 1023
- weights: float32 [9216, 1024], P(('col', 'row')), may hold values from -2.5 to 2.5
Outputs:
- new_covariance: float32 [9216, 9216], P('row', 'col')
- new_weights: float32 [9216, 1024], P(('col', 'row'))
Inputs may be any that keep to these rules, and one draw needn't show every extreme that they name: covariance is symmetric and positive definite.
All inputs are finite; a program needn't handle non-finite values.
Results may differ from a plain program's by a relative error of at most 0.00005.
Values sent between devices are 32-bit elements; how exact they have to be, the bound alone decides.
No kernel may reach another device: no remote copies, remote signals or barrier semaphores. Data moves between devices by JAX's collectives and lax.ppermute only.
A program may use at most 64 MiB of HBM per device.

v0:
```python
import functools

import jax
import jax.numpy as jnp
from jax import lax
from jax.experimental import pallas as pl
from jax.experimental.pallas import tpu as pltpu
from jax.sharding import PartitionSpec as P


HIGHEST = lax.Precision.HIGHEST
HIGH = lax.Precision.HIGH
F32, BF16 = jnp.float32, jnp.bfloat16
LANES = 128
PIVOTS = 4
SMALL = pltpu.CompilerParams(vmem_limit_bytes=20 * 2**20)
VMEM = pl.BlockSpec(memory_space=pltpu.VMEM)


def dot(a, b, dims, precision=HIGHEST):
    return lax.dot_general(a, b, ((dims[:1], dims[1:]), ((), ())), precision=precision, preferred_element_type=F32)


def halves(a):
    high = a.astype(BF16)
    return high, (a - high.astype(F32)).astype(BF16)


def dot3(a, b, dims):
    (ah, al), (bh, bl) = a, b
    return dot(ah, bh, dims, None) + (dot(ah, bl, dims, None) + dot(al, bh, dims, None))


def packs(n, batch):
    return batch == LANES * 3 // 2 and n % 16 == 0


def pack(a):
    n, batch = a.shape
    if not packs(n, batch):
        return a
    tail = a[:, LANES:]
    return jnp.concatenate([a[:, :LANES], jnp.concatenate([tail[: n // 2], tail[n // 2 :]], axis=1)])


def unpack(a, n, batch):
    if not packs(n, batch):
        return a
    tail = a[n:]
    side = LANES // 2
    return jnp.concatenate([a[:n], jnp.concatenate([tail[:, :side], tail[:, side:]])], axis=1)


def inverse_kernel(first, last, s_ref, o_ref):
    n, width = o_ref.shape
    lane = lax.broadcasted_iota(jnp.int32, (1, width), 1)
    sub = lax.broadcasted_iota(jnp.int32, (n, 1), 0)
    if first == 0:
        s = s_ref[...]
        if len(s.shape) == 3:
            s = jnp.concatenate([unpack(s_ref[i], n // 2, n) for i in range(2)])
        if width > n:
            o_ref[:, n:] = jnp.zeros((n, width - n), F32)
        o_ref[:, :n] = 0.5 * (s + s.T)
        o_ref[...] += jnp.where(sub == lane, 1.0, 0.0)
    else:
        o_ref[...] = s_ref[...]

    def step(t, _):
        at = t * PIVOTS
        a = o_ref[...]
        hits = [lane == at + b for b in range(PIVOTS)]
        rows = [o_ref[pl.ds(at + b, 1), :] for b in range(PIVOTS)]
        p = [[jnp.sum(jnp.where(h, r, 0.0), axis=1, keepdims=True) for h in hits] for r in rows]
        cols = [jnp.sum(jnp.where(h, a, 0.0), axis=1, keepdims=True) for h in hits]
        for i in range(PIVOTS):
            inv = 1.0 / p[i][i]
            scaled = [inv if j == i else p[i][j] * inv for j in range(PIVOTS)]
            for o in range(PIVOTS):
                if o != i:
                    f = p[o][i]
                    p[o] = [-f * inv if j == i else p[o][j] - f * scaled[j] for j in range(PIVOTS)]
            p[i] = scaled
        in_lanes = (lane >= at) & (lane < at + PIVOTS)
        in_rows = (sub >= at) & (sub < at + PIVOTS)
        rows = [jnp.where(in_lanes, jnp.where(h, 1.0, 0.0), r) for h, r in zip(hits, rows)]
        out = jnp.where(in_rows | in_lanes, 0.0, a)
        for i in range(PIVOTS):
            new = p[i][0] * rows[0]
            for j in range(1, PIVOTS):
                new = new + p[i][j] * rows[j]
            out = out - jnp.where(in_rows, jnp.where(sub == at + i, -1.0, 0.0), cols[i]) * new
        o_ref[...] = out
        return 0

    lax.fori_loop(first, last, step, 0)


def eliminated(a, n, first, last):
    width = -(-n // LANES) * LANES
    return pl.pallas_call(
        functools.partial(inverse_kernel, first, last),
        out_shape=jax.ShapeDtypeStruct((n, width), F32),
        in_specs=[VMEM],
        out_specs=VMEM,
        compiler_params=SMALL,
        cost_estimate=pl.CostEstimate(flops=2 * n**3, bytes_accessed=8 * n * n, transcendentals=0),
        name="inverse",
    )(a)


def place_kernel(n, place, *refs):
    *piece_refs, high_ref, low_ref = refs
    for i, ref in enumerate(piece_refs):
        at = place[0] ^ i
        high_ref[at], low_ref[at] = halves(unpack(ref[...], n, high_ref.shape[2]))


def placed_halves(pieces, place, n, batch):
    shape = jax.ShapeDtypeStruct((len(pieces), n, batch), BF16)
    return pl.pallas_call(
        functools.partial(place_kernel, n),
        out_shape=(shape, shape),
        grid_spec=pltpu.PrefetchScalarGridSpec(
            num_scalar_prefetch=1, grid=(), in_specs=[VMEM] * len(pieces), out_specs=(VMEM, VMEM)
        ),
        compiler_params=SMALL,
        name="place",
    )(place, *pieces)


def product_kernel(a_ref, b_ref, o_ref):
    o_ref[...] = dot3(halves(a_ref[...]), halves(b_ref[...]), (1, 0))


def product_add_kernel(a_ref, b_ref, c_ref, o_ref):
    o_ref[...] = c_ref[...] + dot3(halves(a_ref[...]), halves(b_ref[...]), (1, 0))


def product(a, b, c=None):
    shape = a.shape[0], b.shape[1]
    return pl.pallas_call(
        product_kernel if c is None else product_add_kernel,
        out_shape=jax.ShapeDtypeStruct(shape, F32),
        in_specs=[VMEM] * (2 if c is None else 3),
        out_specs=VMEM,
        compiler_params=SMALL,
        name="product",
    )(*((a, b) if c is None else (a, b, c)))


def inner_kernel(n, batch, *refs):
    *in_refs, o_ref = refs
    half = len(in_refs) // 2
    inner = 0.0
    for u_ref, x_ref in zip(in_refs[:half], in_refs[half:]):
        inner = inner + dot(unpack(u_ref[...], n, batch), unpack(x_ref[...], n, batch), (0, 0))
    for i in range(2):
        o_ref[i] = pack(inner[i * batch // 2 : (i + 1) * batch // 2])


def inner_of(u, x, n, batch):
    return pl.pallas_call(
        functools.partial(inner_kernel, n, batch),
        out_shape=jax.ShapeDtypeStruct((2, batch * batch // 2 // LANES, LANES), F32),
        in_specs=[VMEM] * (2 * len(u)),
        out_specs=VMEM,
        compiler_params=SMALL,
        name="inner",
    )(*u, *x)


def terms_kernel(n, streams, e, group, place, cov_ref, high_ref, low_ref, o_ref, *scratch):
    pieces, _, batch = high_ref.shape
    packed = n * batch // LANES
    count = o_ref.shape[0] // packed
    at = [pl.ds(pl.multiple_of(((place[2] ^ e) * pieces + (place[1] ^ d)) * n, 8), n) for d in group]
    if streams:
        read_ref, sems = scratch
        copies = [pltpu.make_async_copy(cov_ref.at[at[i], :], read_ref.at[i], sems.at[i]) for i in range(count)]
        for copy in copies:
            copy.start()
    x = [ref[...].reshape(pieces * n, batch) for ref in (high_ref, low_ref)]
    for i in range(count):
        if streams:
            copies[i].wait()
        rows = read_ref[i] if streams else cov_ref[at[i], :]
        o_ref[i * packed : (i + 1) * packed, :] = pack(dot3(halves(rows), x, (1, 0)))


def row_terms(covariance, x_high, x_low, place, e, group, n, streams):
    width, batch = covariance.shape[1], x_high.shape[2]
    count = len(group)
    return pl.pallas_call(
        functools.partial(terms_kernel, n, streams, e, tuple(group)),
        out_shape=jax.ShapeDtypeStruct((count * n * batch // LANES, LANES), F32),
        grid_spec=pltpu.PrefetchScalarGridSpec(
            num_scalar_prefetch=1,
            grid=(),
            in_specs=[pl.BlockSpec(memory_space=pl.ANY) if streams else VMEM, VMEM, VMEM],
            out_specs=VMEM,
            scratch_shapes=[pltpu.VMEM((count, n, width), F32), pltpu.SemaphoreType.DMA((count,))] if streams else [],
        ),
        compiler_params=pltpu.CompilerParams(vmem_limit_bytes=46 * 2**20) if streams else SMALL,
        cost_estimate=pl.CostEstimate(
            flops=6 * count * n * width * batch, bytes_accessed=4 * count * n * width, transcendentals=0
        ),
        name="terms",
    )(place, covariance, x_high, x_low)


def gain_kernel(n, place, inverse_ref, *refs):
    *group_refs, high_ref, low_ref, own_ref, uh_ref, ul_ref = refs
    batch = inverse_ref.shape[0]
    size = n * batch // LANES
    per = group_refs[0].shape[0] // size
    count = len(group_refs) * per
    for i in range(count):
        packed = group_refs[i // per][i % per * size : (i % per + 1) * size, :]
        at = place[1] ^ i
        uh_ref[at], ul_ref[at] = halves(unpack(packed, n, batch))
    inverse = halves(inverse_ref[:, :batch])
    u = [ref[...].reshape(count * n, batch) for ref in (uh_ref, ul_ref)]
    high_ref[...], low_ref[...] = halves(dot3(inverse, u, (1, 1)))
    own_ref[...] = dot3((uh_ref[place[0]], ul_ref[place[0]]), inverse, (1, 0))


def gain_of(inverse, groups, place, n):
    batch = inverse.shape[0]
    count = sum(a.shape[0] for a in groups) // (n * batch // LANES)
    shape = jax.ShapeDtypeStruct((batch, count * n), BF16)
    return pl.pallas_call(
        functools.partial(gain_kernel, n),
        out_shape=(shape, shape, jax.ShapeDtypeStruct((n, batch), F32)),
        grid_spec=pltpu.PrefetchScalarGridSpec(
            num_scalar_prefetch=1,
            grid=(),
            in_specs=[VMEM] * (1 + len(groups)),
            out_specs=(VMEM,) * 3,
            scratch_shapes=[pltpu.VMEM((count, n, batch), BF16)] * 2,
        ),
        compiler_params=SMALL,
        name="gain",
    )(place, inverse, *groups)


def update_kernel(n, place, cov_ref, high_ref, low_ref, *refs):
    *group_refs, o_ref, stage_ref, sems = refs
    batch = high_ref.shape[0]
    size = n * batch // LANES
    per = group_refs[0].shape[0] // size
    pieces = high_ref.shape[1] // n
    gain = high_ref[...], low_ref[...]
    copies = []
    for i in range(len(group_refs) * per):
        block = (place[2] ^ (i // pieces)) * pieces + (place[1] ^ (i % pieces))
        at = pl.ds(pl.multiple_of(block * n, 8), n)
        rows = halves(unpack(group_refs[i // per][i % per * size : (i % per + 1) * size, :], n, batch))
        stage_ref[i] = cov_ref[at, :] - dot3(rows, gain, (1, 0))
        copies.append(pltpu.make_async_copy(stage_ref.at[i], o_ref.at[at, :], sems.at[i]))
        copies[i].start()
    for copy in copies:
        copy.wait()


def updated(covariance, gain_high, gain_low, groups, place, n):
    count, width = covariance.shape[0] // n, covariance.shape[1]
    return pl.pallas_call(
        functools.partial(update_kernel, n),
        out_shape=jax.ShapeDtypeStruct(covariance.shape, F32),
        grid_spec=pltpu.PrefetchScalarGridSpec(
            num_scalar_prefetch=1,
            grid=(),
            in_specs=[VMEM] * (3 + len(groups)),
            out_specs=pl.BlockSpec(memory_space=pl.ANY),
            scratch_shapes=[pltpu.VMEM((count, n, width), F32), pltpu.SemaphoreType.DMA((count,))],
        ),
        compiler_params=SMALL,
        name="update",
    )(place, covariance, gain_high, gain_low, *groups)


def after(a, *others):
    return lax.optimization_barrier((a, *others))[0]


def program(nr, nc):
    k = nc // nr
    assert k == 2

    def swap(a, axis, mask):
        n = nr if axis == "row" else nc
        return lax.ppermute(a, axis, [(i, i ^ mask) for i in range(n)])

    def bits_of(n):
        return [1 << b for b in range(n.bit_length() - 1)]

    masks = bits_of(nr)

    def on_device(covariance, samples, labels, weights):
        row, col = lax.axis_index("row"), lax.axis_index("col")
        z, x = lax.div(col, k), lax.rem(col, k)
        place = jnp.stack([row, z, x]).astype(jnp.int32)
        batch, piece = samples.shape
        fits = packs(piece, batch)

        first_of = {m: (row & m) == 0 for m in masks}
        handed_to = {m: ((row ^ z) & m) != 0 for m in masks}

        def ordered(low, mine, other):
            return jnp.where(low, mine, other), jnp.where(low, other, mine)

        xt = pack(samples.T)
        size = xt.shape[0]
        x_by = {0: xt}
        for mask in reversed(masks):
            for d in list(x_by):
                x_by[d | mask] = swap(x_by[d], "row", mask)
        order = list(reversed(range(nr)))
        groups = [order[: nr // 2], order[nr // 2 :]]

        if fits:
            x_high, x_low = placed_halves([x_by[d] for d in range(nr)], place, piece, batch)
            placed = x_high

            def terms_of(e, group, x_high):
                return row_terms(covariance, x_high, x_low, place, e, group, piece, e == 1 and group is groups[0])
        else:
            placed = jnp.concatenate([x_by[0]] * nr)
            for d in range(nr):
                placed = lax.dynamic_update_slice_in_dim(placed, x_by[d], (row ^ d) * piece, 0)
            whole = dot(covariance, placed, (1, 0), HIGH)

            def terms_of(e, group, _):
                at = [((x ^ e) * nr + (z ^ d)) * piece for d in group]
                return jnp.concatenate([lax.dynamic_slice_in_dim(whole, i, piece, 0) for i in at])

        predicted = product(samples, weights) if fits else dot(samples, weights, (1, 0))
        sends = [("row", row, m, True) for m in masks] + [("col", z, m * k, False) for m in masks]
        sends += [("col", x, 1, False)]

        def step_on(predicted, *others):
            axis, index, mask, halves_it = sends.pop(0)
            if halves_it:
                n = predicted.shape[0] // 2
                low = (index & mask) == 0
                a, b = predicted[:n], predicted[n:]
                keep, give = jnp.where(low, a, b), jnp.where(low, b, a)
            else:
                keep = give = predicted
            got = swap(give, axis, mask)
            predicted = keep + got
            return tuple(lax.optimization_barrier((predicted, *others)))

        transposed = [
            (z_ * nc + k * r_ + x_, r_ * nc + k * z_ + x_) for r_ in range(nr) for z_ in range(nr) for x_ in range(k)
        ]
        made, kept = [], []
        predicted, placed, first_of, handed_to = lax.optimization_barrier((predicted, placed, first_of, handed_to))
        made.append(terms_of(1, groups[0], placed))
        predicted, placed = step_on(predicted, placed)
        predicted = after(predicted, made[0])
        x_piece = lax.ppermute(after(xt, made[0]), ("row", "col"), transposed)
        made.append(terms_of(1, groups[1], placed))
        predicted, placed = step_on(predicted, placed)
        predicted = after(predicted, made[1])
        kept.append(terms_of(0, groups[0], placed))
        predicted, placed, x_piece = step_on(predicted, placed, x_piece)
        predicted = after(predicted, kept[0])
        kept.append(terms_of(0, groups[1], placed))
        sent = []
        for a in made:
            sent.append(swap(a, "col", 1))
        while len(sends) > 1:
            predicted, sent[0], kept[1] = step_on(predicted, sent[0], kept[1])
        x_far = swap(after(x_piece, kept[1]), "col", masks[-1] * k)
        predicted, sent[1] = lax.optimization_barrier((predicted, sent[1]))

        part = {}
        for group, a, b in zip(groups, kept, sent):
            for i, d in enumerate(group):
                part[d] = a[i * size : (i + 1) * size] + b[i * size : (i + 1) * size]
        for mask in masks[:-1]:
            for d in sorted(part, reverse=True):
                if d & mask:
                    got = swap(part.pop(d), "col", mask * k)
                    part[d ^ mask] = part[d ^ mask] + got
        last = masks[-1]
        predicted, part[0] = step_on(predicted, part[0])
        got = swap(part[last], "col", last * k)

        if fits:
            inner = inner_of([part[0], part[last]], [x_piece, x_far], piece, batch)
        else:
            inner = (dot(part[0], x_piece, (0, 0)) + dot(part[last], x_far, (0, 0))).reshape(2, batch // 2, batch)
        low = first_of[1]
        inner = jnp.where(low, inner[0], inner[1]) + swap(jnp.where(low, inner[1], inner[0]), "row", 1)
        for mask in masks[1:]:
            inner = inner + swap(inner, "row", mask)
        for mask in bits_of(k):
            hop = swap(inner, "col", mask)
            inner = inner + hop
        u_piece = part[0] + got
        for mask in reversed(masks):
            predicted = jnp.concatenate(ordered(first_of[mask], predicted, swap(predicted, "row", mask)))
            if mask > 1:
                predicted, u_piece = lax.optimization_barrier((predicted, u_piece))
        for mask in masks:
            inner = inner + swap(inner, "col", mask * k)
        inner = jnp.stack(ordered(low, inner, swap(inner, "row", 1)))
        if not fits:
            inner = inner.reshape(batch, batch)

        u_by = {0: u_piece}
        for d in range(1, nr):
            u_by[d] = swap(u_piece, "col", d * k)
        own = [jnp.concatenate([u_by[d] for d in range(nr // 2)])]
        peer = [swap(own[0], "col", 1)]

        def handed(a, mask):
            pairs = [
                (r_ * nc + c_, (r_ ^ mask) * nc + c_)
                for c_ in range(nc)
                for r_ in range(nr)
                if (r_ ^ (c_ // k)) & (2 * mask - 1) == 0
            ]
            return jnp.where(handed_to[mask], lax.ppermute(a, ("row", "col"), pairs), a)

        steps = batch // PIVOTS
        near = own[0]
        for mask in reversed(masks[1:]):
            near = handed(near, mask)
        inverse = eliminated(inner, batch, 0, steps // 3)
        inverse, near = lax.optimization_barrier((inverse, near))
        near = handed(near, 1)
        inverse = eliminated(inverse, batch, steps // 3, 2 * steps // 3)
        inverse, *far = lax.optimization_barrier((inverse, *(u_by[d] for d in range(nr // 2, nr))))
        own.append(jnp.concatenate(far))
        peer.append(swap(own[1], "col", 1))
        far = own[1]
        for mask in reversed(masks):
            far = handed(far, mask)
        inverse = eliminated(inverse, batch, 2 * steps // 3, steps)
        u_cols = [near, far]

        classes = lax.broadcasted_iota(jnp.int32, (batch, weights.shape[1]), 1)
        missed = (labels[:, None] == classes).astype(F32) - predicted
        if fits:
            gain_high, gain_low, gain_piece = gain_of(inverse, u_cols, place, piece)
            new_covariance = updated(covariance, gain_high, gain_low, own + peer, place, piece)
            new_weights = product(gain_piece, missed, weights)
        else:

            def in_order(pieces):
                joined = jnp.concatenate(pieces)
                out = joined
                for d in range(nr):
                    got = joined[d * piece : (d + 1) * piece]
                    out = lax.dynamic_update_slice_in_dim(out, got, (z ^ d) * piece, 0)
                return out

            gain = dot(in_order(u_cols), inverse[:, :batch], (1, 0))
            gain_piece = lax.dynamic_slice_in_dim(gain, row * piece, piece, 0)
            u_rows = jnp.concatenate(ordered(x == 0, in_order(own), in_order(peer)))
            new_covariance = covariance - dot(u_rows, gain, (1, 1), HIGH)
            new_weights = weights + dot(gain_piece, missed, (1, 0))
        return new_covariance, new_weights

    return on_device


def solution(mesh):
    on_device = program(mesh.shape["row"], mesh.shape["col"])

    return jax.shard_map(
        on_device,
        mesh=mesh,
        in_specs=(P("row", "col"), P(None, ("col", "row")), P(), P(("col", "row"), None)),
        out_specs=(P("row", "col"), P(("col", "row"), None)),
        check_vma=False,
    )
```

profile of v0, /device:TPU:11, one launch (start us, length us, event | category | flops | bytes accessed | tf_op | source)
XLA Modules:
  0.0 149.2 jit_solution(6029935070129791081)
XLA Ops:
  0.6 1.1 copy.6
  1.9 1.3 collective-permute-start.1
  4.1 4.1 %collective-permute-done.1.refs_2_ = f32[432,128]{1,0:T(8,128)S(1)} collective-permute-done((f32[432,128]{1,0:T(8,128)S(1)}, f32[432,128]{1,0:T(8,128)S(1)}, u32[]{:S(2)}, u32[]{:S(2)}) %collective-permute-start.1) | collective-permute-done | bytes 221216 | tf_op jit(solution)/shard_map/ppermute | solution.py:293
  8.2 1.5 %collective-permute-start.2 = (f32[432,128]{1,0:T(8,128)S(1)}, f32[432,128]{1,0:T(8,128)S(1)}, u32[]{:S(2)}, u32[]{:S(2)}) collective-permute-start(f32[432,128]{1,0:T(8,128)S(1)} %collective-permute-done.1.refs_2_), channel_id=1, source_target_pairs={{0,8},{8,0},{16,24},{24,16},{1,9},{9,1},{17,25},{25,17},{2,10},{10... | collective-permute-start | bytes 663560 | tf_op jit(solution)/shard_map/ppermute | solution.py:293
  9.8 1.3 copy-done.1
  11.1 1.0 copy-done.3
  13.8 5.2 %terms.4 = f32[864,128]{1,0:T(8,128)S(1)} custom-call(s32[3]{0:T(128)S(1)} %pad_add_fusion.place, f32[2304,1152]{1,0:T(8,128)} %cov_ref.9, bf16[4,288,192]{2,1,0:T(8,128)(2,1)S(1)} %get-tuple-element.53.high_ref, bf16[4,288,192]{2,1,0:T(8,128)(2,1)S(1)} %get-tuple-element.44.low_ref), custom_call_target="tpu_custom_call" | custom-call | flops 764411904 | bytes 2654208 | tf_op jit(solution)/shard_map/terms/pallas_call | solution.py:194
  19.1 1.3 collective-permute-start.4
  21.4 1.9 %terms.5 = f32[864,128]{1,0:T(8,128)S(1)} custom-call(s32[3]{0:T(128)S(1)} %pad_add_fusion.place, f32[2304,1152]{1,0:T(8,128)S(1)} %copy-done, bf16[4,288,192]{2,1,0:T(8,128)(2,1)S(1)} %get-tuple-element.53.high_ref, bf16[4,288,192]{2,1,0:T(8,128)(2,1)S(1)} %get-tuple-element.44.low_ref), custom_call_target="tpu_custom_call" | custom-call | flops 764411904 | bytes 2654208 | tf_op jit(solution)/shard_map/terms/pallas_call | solution.py:194
  23.3 1.3 collective-permute-start.9
  25.0 3.4 %collective-permute-start.5 = (f32[48,1024]{1,0:T(8,128)S(1)}, f32[48,1024]{1,0:T(8,128)S(1)}, u32[]{:S(2)}, u32[]{:S(2)}) collective-permute-start(f32[48,1024]{1,0:T(8,128)S(1)} %select_add_fusion.1), channel_id=1, source_target_pairs={{0,2},{1,3},{2,0},{3,1},{4,6},{5,7},{6,4},{7,5},{8,10},{9,11},{10,... | collective-permute-start | bytes 589832 | tf_op jit(solution)/shard_map/ppermute | solution.py:293
  28.4 1.9 %terms.6 = f32[864,128]{1,0:T(8,128)S(1)} custom-call(s32[3]{0:T(128)S(1)} %pad_add_fusion.place, f32[2304,1152]{1,0:T(8,128)S(1)} %copy-done, bf16[4,288,192]{2,1,0:T(8,128)(2,1)S(1)} %get-tuple-element.53.high_ref, bf16[4,288,192]{2,1,0:T(8,128)(2,1)S(1)} %get-tuple-element.44.low_ref), custom_call_target="tpu_custom_call" | custom-call | flops 764411904 | bytes 2654208 | tf_op jit(solution)/shard_map/terms/pallas_call | solution.py:194
  30.4 5.9 %collective-permute-done.5 = f32[48,1024]{1,0:T(8,128)S(1)} collective-permute-done((f32[48,1024]{1,0:T(8,128)S(1)}, f32[48,1024]{1,0:T(8,128)S(1)}, u32[]{:S(2)}, u32[]{:S(2)}) %collective-permute-start.5) | collective-permute-done | bytes 196640 | tf_op jit(solution)/shard_map/ppermute | solution.py:293
  36.3 1.8 %collective-permute-start.7 = (f32[48,1024]{1,0:T(8,128)S(1)}, f32[48,1024]{1,0:T(8,128)S(1)}, u32[]{:S(2)}, u32[]{:S(2)}) collective-permute-start(f32[48,1024]{1,0:T(8,128)S(1)} %add.53), channel_id=1, source_target_pairs={{0,4},{1,5},{2,6},{3,7},{4,0},{5,1},{6,2},{7,3},{8,12},{9,13},{10,... | collective-permute-start | bytes 589832 | tf_op jit(solution)/shard_map/ppermute | solution.py:293
  38.1 1.9 %terms.7 = f32[864,128]{1,0:T(8,128)S(1)} custom-call(s32[3]{0:T(128)S(1)} %pad_add_fusion.place, f32[2304,1152]{1,0:T(8,128)S(1)} %copy-done, bf16[4,288,192]{2,1,0:T(8,128)(2,1)S(1)} %get-tuple-element.53.high_ref, bf16[4,288,192]{2,1,0:T(8,128)(2,1)S(1)} %get-tuple-element.44.low_ref), custom_call_target="tpu_custom_call" | custom-call | flops 764411904 | bytes 2654208 | tf_op jit(solution)/shard_map/terms/pallas_call | solution.py:194
  40.1 5.9 %collective-permute-done.7 = f32[48,1024]{1,0:T(8,128)S(1)} collective-permute-done((f32[48,1024]{1,0:T(8,128)S(1)}, f32[48,1024]{1,0:T(8,128)S(1)}, u32[]{:S(2)}, u32[]{:S(2)}) %collective-permute-start.7) | collective-permute-done | bytes 196640 | tf_op jit(solution)/shard_map/ppermute | solution.py:293
  46.0 1.3 collective-permute-start.10
  47.3 3.2 %collective-permute-start.11 = (f32[432,128]{1,0:T(8,128)S(1)}, f32[432,128]{1,0:T(8,128)S(1)}, u32[]{:S(2)}, u32[]{:S(2)}) collective-permute-start(f32[432,128]{1,0:T(8,128)S(1)} %slice_add_fusion.2), channel_id=1, source_target_pairs={{0,2},{1,3},{2,0},{3,1},{4,6},{5,7},{6,4},{7,5},{8,10},{9,11},{10,... | collective-permute-start | bytes 663560 | tf_op jit(solution)/shard_map/ppermute | solution.py:293
  50.6 1.1 collective-permute-start.13
  51.7 1.0 collective-permute-done.10
  52.7 6.6 %collective-permute-done.11 = f32[432,128]{1,0:T(8,128)S(1)} collective-permute-done((f32[432,128]{1,0:T(8,128)S(1)}, f32[432,128]{1,0:T(8,128)S(1)}, u32[]{:S(2)}, u32[]{:S(2)}) %collective-permute-start.11) | collective-permute-done | bytes 221216 | tf_op jit(solution)/shard_map/ppermute | solution.py:293
  59.4 4.7 %collective-permute-done.12 = f32[432,128]{1,0:T(8,128)S(1)} collective-permute-done((f32[432,128]{1,0:T(8,128)S(1)}, f32[432,128]{1,0:T(8,128)S(1)}, u32[]{:S(2)}, u32[]{:S(2)}) %collective-permute-start.12) | collective-permute-done | bytes 221216 | tf_op jit(solution)/shard_map/ppermute | solution.py:293
  64.8 1.0 inner.1
  65.9 1.3 collective-permute-start.14
  67.1 1.5 %collective-permute-start.21 = (f32[432,128]{1,0:T(8,128)S(1)}, f32[432,128]{1,0:T(8,128)S(1)}, u32[]{:S(2)}, u32[]{:S(2)}) collective-permute-start(f32[432,128]{1,0:T(8,128)S(1)} %fusion.refs_1_), channel_id=1, source_target_pairs={{0,4},{1,5},{2,6},{3,7},{4,0},{5,1},{6,2},{7,3},{8,12},{9,13},{10,... | collective-permute-start | bytes 663560 | tf_op jit(solution)/shard_map/ppermute | solution.py:293
  68.7 2.5 %collective-permute-start.20 = (f32[48,1024]{1,0:T(8,128)S(1)}, f32[48,1024]{1,0:T(8,128)S(1)}, u32[]{:S(2)}, u32[]{:S(2)}) collective-permute-start(f32[48,1024]{1,0:T(8,128)S(1)} %add.55), channel_id=1, source_target_pairs={{0,16},{8,24},{16,0},{24,8},{1,17},{9,25},{17,1},{25,9},{2,18},{10... | collective-permute-start | bytes 589832 | tf_op jit(solution)/shard_map/ppermute | solution.py:293
  71.3 4.8 %collective-permute-done.20 = f32[48,1024]{1,0:T(8,128)S(1)} collective-permute-done((f32[48,1024]{1,0:T(8,128)S(1)}, f32[48,1024]{1,0:T(8,128)S(1)}, u32[]{:S(2)}, u32[]{:S(2)}) %collective-permute-start.20) | collective-permute-done | bytes 196640 | tf_op jit(solution)/shard_map/ppermute | solution.py:293
  76.2 1.9 %collective-permute-done.21 = f32[432,128]{1,0:T(8,128)S(1)} collective-permute-done((f32[432,128]{1,0:T(8,128)S(1)}, f32[432,128]{1,0:T(8,128)S(1)}, u32[]{:S(2)}, u32[]{:S(2)}) %collective-permute-start.21) | collective-permute-done | bytes 221216 | tf_op jit(solution)/shard_map/ppermute | solution.py:293
  78.1 3.3 %collective-permute-start.22 = (f32[432,128]{1,0:T(8,128)S(1)}, f32[432,128]{1,0:T(8,128)S(1)}, u32[]{:S(2)}, u32[]{:S(2)}) collective-permute-start(f32[432,128]{1,0:T(8,128)S(1)} %add.67), channel_id=1, source_target_pairs={{0,2},{1,3},{2,0},{3,1},{4,6},{5,7},{6,4},{7,5},{8,10},{9,11},{10,... | collective-permute-start | bytes 663560 | tf_op jit(solution)/shard_map/ppermute | solution.py:293
  81.9 3.1 %collective-permute-done.16 = f32[144,128]{1,0:T(8,128)S(1)} collective-permute-done((f32[144,128]{1,0:T(8,128)S(1)}, f32[144,128]{1,0:T(8,128)S(1)}, u32[]{:S(2)}, u32[]{:S(2)}) %collective-permute-start.16) | collective-permute-done | bytes 73760 | tf_op jit(solution)/shard_map/ppermute | solution.py:293
  85.2 3.2 %collective-permute-done.17 = f32[144,128]{1,0:T(8,128)S(1)} collective-permute-done((f32[144,128]{1,0:T(8,128)S(1)}, f32[144,128]{1,0:T(8,128)S(1)}, u32[]{:S(2)}, u32[]{:S(2)}) %collective-permute-start.17) | collective-permute-done | bytes 73760 | tf_op jit(solution)/shard_map/ppermute | solution.py:293
  88.3 1.0 collective-permute-start.18
  89.4 4.1 %collective-permute-start.23 = (f32[864,128]{1,0:T(8,128)S(1)}, f32[864,128]{1,0:T(8,128)S(1)}, u32[]{:S(2)}, u32[]{:S(2)}) collective-permute-start(f32[864,128]{1,0:T(8,128)S(1)} %constant_dynamic-update-slice_fusion.refs_0_), channel_id=1, source_target_pairs={{0,16},{1,17},{10,26},{11,27},{20,4},{21,5},{30,14},{31,15}} | collective-permute-start | bytes 1327112 | tf_op jit(solution)/shard_map/ppermute | solution.py:427
  93.5 2.9 %collective-permute-start.19 = (f32[144,128]{1,0:T(8,128)S(1)}, f32[144,128]{1,0:T(8,128)S(1)}, u32[]{:S(2)}, u32[]{:S(2)}) collective-permute-start(f32[144,128]{1,0:T(8,128)S(1)} %add.66), channel_id=1, source_target_pairs={{0,8},{8,0},{16,24},{24,16},{1,9},{9,1},{17,25},{25,17},{2,10},{10... | collective-permute-start | bytes 221192 | tf_op jit(solution)/shard_map/ppermute | solution.py:293
  96.5 1.7 %collective-permute-start.25 = (f32[432,128]{1,0:T(8,128)S(1)}, f32[432,128]{1,0:T(8,128)S(1)}, u32[]{:S(2)}, u32[]{:S(2)}) collective-permute-start(f32[432,128]{1,0:T(8,128)S(1)} %add.67), channel_id=1, source_target_pairs={{0,6},{1,7},{2,4},{3,5},{4,2},{5,3},{6,0},{7,1},{8,14},{9,15},{10,... | collective-permute-start | bytes 663560 | tf_op jit(solution)/shard_map/ppermute | solution.py:293
  98.9 4.4 %inverse.3.s_ref = f32[192,256]{1,0:T(8,128)S(1)} custom-call(f32[2,144,128]{2,1,0:T(8,128)S(1)} %pad_maximum_fusion.1.s_ref), custom_call_target="tpu_custom_call" | custom-call | flops 14155776 | bytes 294912 | tf_op jit(solution)/shard_map/inverse/pallas_call | solution.py:101
  103.4 4.2 %inverse.4.s_ref = f32[192,256]{1,0:T(8,128)S(1)} custom-call(f32[192,256]{1,0:T(8,128)S(1)} %inverse.3.s_ref), custom_call_target="tpu_custom_call" | custom-call | flops 14155776 | bytes 294912 | tf_op jit(solution)/shard_map/inverse/pallas_call | solution.py:101
  107.6 3.1 %collective-permute-done.24 = f32[432,128]{1,0:T(8,128)S(1)} collective-permute-done((f32[432,128]{1,0:T(8,128)S(1)}, f32[432,128]{1,0:T(8,128)S(1)}, u32[]{:S(2)}, u32[]{:S(2)}) %collective-permute-start.24) | collective-permute-done | bytes 221216 | tf_op jit(solution)/shard_map/ppermute | solution.py:293
  110.7 7.2 %collective-permute-done.25 = f32[432,128]{1,0:T(8,128)S(1)} collective-permute-done((f32[432,128]{1,0:T(8,128)S(1)}, f32[432,128]{1,0:T(8,128)S(1)}, u32[]{:S(2)}, u32[]{:S(2)}) %collective-permute-start.25) | collective-permute-done | bytes 221216 | tf_op jit(solution)/shard_map/ppermute | solution.py:293
  118.0 3.2 %collective-permute-start.27 = (f32[864,128]{1,0:T(8,128)S(1)}, f32[864,128]{1,0:T(8,128)S(1)}, u32[]{:S(2)}, u32[]{:S(2)}) collective-permute-start(f32[864,128]{1,0:T(8,128)S(1)} %constant_dynamic-update-slice_fusion.2.refs_1_), channel_id=1, source_target_pairs={{0,16},{1,17},{10,26},{11,27},{20,4},{21,5},{30,14},{31,15}} | collective-permute-start | bytes 1327112 | tf_op jit(solution)/shard_map/ppermute | solution.py:427
  121.3 1.3 collective-permute-start.26
  122.6 3.7 %collective-permute-done.27 = f32[864,128]{1,0:T(8,128)S(1)} collective-permute-done((f32[864,128]{1,0:T(8,128)S(1)}, f32[864,128]{1,0:T(8,128)S(1)}, u32[]{:S(2)}, u32[]{:S(2)}) %collective-permute-start.27) | collective-permute-done | bytes 442400 | tf_op jit(solution)/shard_map/ppermute | solution.py:427
  126.4 1.5 %collective-permute-start.28 = (f32[864,128]{1,0:T(8,128)S(1)}, f32[864,128]{1,0:T(8,128)S(1)}, u32[]{:S(2)}, u32[]{:S(2)}) collective-permute-start(f32[864,128]{1,0:T(8,128)S(1)} %broadcast_select_fusion.2), channel_id=1, source_target_pairs={{0,8},{16,24},{1,9},{17,25},{10,2},{26,18},{11,3},{27,19},{4,12},{... | collective-permute-start | bytes 1327112 | tf_op jit(solution)/shard_map/ppermute | solution.py:427
  128.2 4.3 %inverse.5.inverse_ref = f32[192,256]{1,0:T(8,128)S(1)} custom-call(f32[192,256]{1,0:T(8,128)S(1)} %inverse.4.s_ref), custom_call_target="tpu_custom_call" | custom-call | flops 14155776 | bytes 294912 | tf_op jit(solution)/shard_map/inverse/pallas_call | solution.py:101
  132.6 1.5 %gain.1 = (bf16[192,1152]{1,0:T(8,128)(2,1)S(1)}, bf16[192,1152]{1,0:T(8,128)(2,1)S(1)}, f32[288,192]{1,0:T(8,128)S(1)}) custom-call(s32[3]{0:T(128)S(1)} %pad_add_fusion.place, f32[192,256]{1,0:T(8,128)S(1)} %inverse.5.inverse_ref, f32[864,128]{1,0:T(8,128)S(1)} %broadcast_select_fusion.1.refs_0_, f32[864,128]{1,0:T(8,128)S(1)} %broadcast_select_fusion.refs_1_), custom_call_target="tpu_custom_call" | custom-call | tf_op jit(solution)/shard_map/gain/pallas_call | solution.py:232
  134.1 1.7 %product.3 = f32[288,1024]{1,0:T(8,128)} custom-call(f32[288,192]{1,0:T(8,128)S(1)} %get-tuple-element.74.a_ref, f32[192,1024]{1,0:T(8,128)S(1)} %maximum_subtract_fusion.b_ref, f32[288,1024]{1,0:T(8,128)S(1)} %copy-done.2), custom_call_target="tpu_custom_call" | custom-call | tf_op jit(solution)/shard_map/product/pallas_call | solution.py:142
  135.8 5.7 %collective-permute-done.30.refs_3_ = f32[864,128]{1,0:T(8,128)S(1)} collective-permute-done((f32[864,128]{1,0:T(8,128)S(1)}, f32[864,128]{1,0:T(8,128)S(1)}, u32[]{:S(2)}, u32[]{:S(2)}) %collective-permute-start.30) | collective-permute-done | bytes 442400 | tf_op jit(solution)/shard_map/ppermute | solution.py:293
  141.5 7.5 %update.1 = f32[2304,1152]{1,0:T(8,128)} custom-call(s32[3]{0:T(128)S(1)} %pad_add_fusion.place, f32[2304,1152]{1,0:T(8,128)S(1)} %copy-done, bf16[192,1152]{1,0:T(8,128)(2,1)S(1)} %get-tuple-element.72.high_ref, bf16[192,1152]{1,0:T(8,128)(2,1)S(1)} %get-tuple-element.73.low_ref, f32[864,128]{1,0:T(8,128)S(1)} %constant_dynamic-update-slice_fusion.refs_0_, ...), custom_call_target="tpu_custom_call" | custom-call | tf_op jit(solution)/shard_map/update/pallas_call | solution.py:268
  (76 shorter events, 7.5 us)
Async XLA Ops:
  1.9 6.4 %collective-permute-start.1 = (f32[432,128]{1,0:T(8,128)S(1)}, f32[432,128]{1,0:T(8,128)S(1)}, u32[]{:S(2)}, u32[]{:S(2)}) collective-permute-start(f32[432,128]{1,0:T(8,128)S(1)} %maximum_maximum_fusion.refs_0_), channel_id=1, source_target_pairs={{0,16},{8,24},{16,0},{24,8},{1,17},{9,25},{17,1},{25,9},{2,18},{10... | collective-permute-start | bytes 663560 | tf_op jit(solution)/shard_map/ppermute | solution.py:293
  3.2 9.7 %collective-permute-start = (f32[432,128]{1,0:T(8,128)S(1)}, f32[432,128]{1,0:T(8,128)S(1)}, u32[]{:S(2)}, u32[]{:S(2)}) collective-permute-start(f32[432,128]{1,0:T(8,128)S(1)} %maximum_maximum_fusion.refs_0_), channel_id=1, source_target_pairs={{0,8},{8,0},{16,24},{24,16},{1,9},{9,1},{17,25},{25,17},{2,10},{10... | collective-permute-start | bytes 663560 | tf_op jit(solution)/shard_map/ppermute | solution.py:293
  8.2 4.7 %collective-permute-start.2 = (f32[432,128]{1,0:T(8,128)S(1)}, f32[432,128]{1,0:T(8,128)S(1)}, u32[]{:S(2)}, u32[]{:S(2)}) collective-permute-start(f32[432,128]{1,0:T(8,128)S(1)} %collective-permute-done.1.refs_2_), channel_id=1, source_target_pairs={{0,8},{8,0},{16,24},{24,16},{1,9},{9,1},{17,25},{25,17},{2,10},{10... | collective-permute-start | bytes 663560 | tf_op jit(solution)/shard_map/ppermute | solution.py:293
  9.8 1.3 copy-start.1
  11.1 1.0 copy-start.3
  12.8 8.5 %copy-start = (f32[2304,1152]{1,0:T(8,128)S(1)}, f32[2304,1152]{1,0:T(8,128)}, u32[]{:S(2)}) copy-start(f32[2304,1152]{1,0:T(8,128)} %cov_ref.9) | copy-start | bytes 31850500
  13.7 5.3 %collective-permute-start.3 = (f32[96,1024]{1,0:T(8,128)S(1)}, f32[96,1024]{1,0:T(8,128)S(1)}, u32[]{:S(2)}, u32[]{:S(2)}) collective-permute-start(f32[96,1024]{1,0:T(8,128)S(1)} %slice_select_fusion), channel_id=1, source_target_pairs={{0,8},{8,0},{16,24},{24,16},{1,9},{9,1},{17,25},{25,17},{2,10},{10... | collective-permute-start | bytes 1179656 | tf_op jit(solution)/shard_map/ppermute | solution.py:293
  19.1 5.9 %collective-permute-start.4 = (f32[48,1024]{1,0:T(8,128)S(1)}, f32[48,1024]{1,0:T(8,128)S(1)}, u32[]{:S(2)}, u32[]{:S(2)}) collective-permute-start(f32[48,1024]{1,0:T(8,128)S(1)} %slice_select_fusion.1), channel_id=1, source_target_pairs={{0,16},{8,24},{16,0},{24,8},{1,17},{9,25},{17,1},{25,9},{2,18},{10... | collective-permute-start | bytes 589832 | tf_op jit(solution)/shard_map/ppermute | solution.py:293
  20.4 25.6 %collective-permute-start.8 = (f32[864,128]{1,0:T(8,128)S(1)}, f32[864,128]{1,0:T(8,128)S(1)}, u32[]{:S(2)}, u32[]{:S(2)}) collective-permute-start(f32[864,128]{1,0:T(8,128)S(1)} %terms.4), channel_id=1, source_target_pairs={{0,1},{1,0},{2,3},{3,2},{4,5},{5,4},{6,7},{7,6},{8,9},{9,8},{10,11... | collective-permute-start | bytes 1327112 | tf_op jit(solution)/shard_map/ppermute | solution.py:293
  20.7 15.6 %collective-permute-start.6 = (f32[432,128]{1,0:T(8,128)S(1)}, f32[432,128]{1,0:T(8,128)S(1)}, u32[]{:S(2)}, u32[]{:S(2)}) collective-permute-start(f32[432,128]{1,0:T(8,128)S(1)} %maximum_maximum_fusion.refs_0_), channel_id=1, source_target_pairs={{0,0},{1,1},{8,2},{9,3},{16,4},{17,5},{24,6},{25,7},{2,8},{3,9},{1... | collective-permute-start | bytes 663560 | tf_op jit(solution)/shard_map/ppermute | solution.py:363
  23.3 22.7 %collective-permute-start.9 = (f32[864,128]{1,0:T(8,128)S(1)}, f32[864,128]{1,0:T(8,128)S(1)}, u32[]{:S(2)}, u32[]{:S(2)}) collective-permute-start(f32[864,128]{1,0:T(8,128)S(1)} %terms.5), channel_id=1, source_target_pairs={{0,1},{1,0},{2,3},{3,2},{4,5},{5,4},{6,7},{7,6},{8,9},{9,8},{10,11... | collective-permute-start | bytes 1327112 | tf_op jit(solution)/shard_map/ppermute | solution.py:293
  25.0 11.2 %collective-permute-start.5 = (f32[48,1024]{1,0:T(8,128)S(1)}, f32[48,1024]{1,0:T(8,128)S(1)}, u32[]{:S(2)}, u32[]{:S(2)}) collective-permute-start(f32[48,1024]{1,0:T(8,128)S(1)} %select_add_fusion.1), channel_id=1, source_target_pairs={{0,2},{1,3},{2,0},{3,1},{4,6},{5,7},{6,4},{7,5},{8,10},{9,11},{10,... | collective-permute-start | bytes 589832 | tf_op jit(solution)/shard_map/ppermute | solution.py:293
  36.3 9.6 %collective-permute-start.7 = (f32[48,1024]{1,0:T(8,128)S(1)}, f32[48,1024]{1,0:T(8,128)S(1)}, u32[]{:S(2)}, u32[]{:S(2)}) collective-permute-start(f32[48,1024]{1,0:T(8,128)S(1)} %add.53), channel_id=1, source_target_pairs={{0,4},{1,5},{2,6},{3,7},{4,0},{5,1},{6,2},{7,3},{8,12},{9,13},{10,... | collective-permute-start | bytes 589832 | tf_op jit(solution)/shard_map/ppermute | solution.py:293
  40.0 87.9 %copy-start.4 = (s32[192]{0:T(256)S(1)}, s32[192]{0:T(256)}, u32[]{:S(2)}) copy-start(s32[192]{0:T(256)} %param.6) | copy-start | bytes 2308
  46.0 88.2 %copy-start.2 = (f32[288,1024]{1,0:T(8,128)S(1)}, f32[288,1024]{1,0:T(8,128)}, u32[]{:S(2)}) copy-start(f32[288,1024]{1,0:T(8,128)} %c_ref.1) | copy-start | bytes 3538948
  46.0 6.7 %collective-permute-start.10 = (f32[48,1024]{1,0:T(8,128)S(1)}, f32[48,1024]{1,0:T(8,128)S(1)}, u32[]{:S(2)}, u32[]{:S(2)}) collective-permute-start(f32[48,1024]{1,0:T(8,128)S(1)} %add.54), channel_id=1, source_target_pairs={{0,1},{1,0},{2,3},{3,2},{4,5},{5,4},{6,7},{7,6},{8,9},{9,8},{10,11... | collective-permute-start | bytes 589832 | tf_op jit(solution)/shard_map/ppermute | solution.py:293
  47.3 12.0 %collective-permute-start.11 = (f32[432,128]{1,0:T(8,128)S(1)}, f32[432,128]{1,0:T(8,128)S(1)}, u32[]{:S(2)}, u32[]{:S(2)}) collective-permute-start(f32[432,128]{1,0:T(8,128)S(1)} %slice_add_fusion.2), channel_id=1, source_target_pairs={{0,2},{1,3},{2,0},{3,1},{4,6},{5,7},{6,4},{7,5},{8,10},{9,11},{10,... | collective-permute-start | bytes 663560 | tf_op jit(solution)/shard_map/ppermute | solution.py:293
  50.5 13.5 %collective-permute-start.12 = (f32[432,128]{1,0:T(8,128)S(1)}, f32[432,128]{1,0:T(8,128)S(1)}, u32[]{:S(2)}, u32[]{:S(2)}) collective-permute-start(f32[432,128]{1,0:T(8,128)S(1)} %slice_add_fusion), channel_id=1, source_target_pairs={{0,2},{1,3},{2,0},{3,1},{4,6},{5,7},{6,4},{7,5},{8,10},{9,11},{10,... | collective-permute-start | bytes 663560 | tf_op jit(solution)/shard_map/ppermute | solution.py:293
  50.6 14.2 %collective-permute-start.13 = (f32[432,128]{1,0:T(8,128)S(1)}, f32[432,128]{1,0:T(8,128)S(1)}, u32[]{:S(2)}, u32[]{:S(2)}) collective-permute-start(f32[432,128]{1,0:T(8,128)S(1)} %collective-permute-done.6.refs_2_), channel_id=1, source_target_pairs={{0,4},{1,5},{2,6},{3,7},{4,0},{5,1},{6,2},{7,3},{8,12},{9,13},{10,... | collective-permute-start | bytes 663560 | tf_op jit(solution)/shard_map/ppermute | solution.py:293
  65.9 5.3 %collective-permute-start.14 = (f32[144,128]{1,0:T(8,128)S(1)}, f32[144,128]{1,0:T(8,128)S(1)}, u32[]{:S(2)}, u32[]{:S(2)}) collective-permute-start(f32[144,128]{1,0:T(8,128)S(1)} %select_bitcast_fusion.2), channel_id=1, source_target_pairs={{0,8},{8,0},{16,24},{24,16},{1,9},{9,1},{17,25},{25,17},{2,10},{10... | collective-permute-start | bytes 221192 | tf_op jit(solution)/shard_map/ppermute | solution.py:293
  67.1 11.0 %collective-permute-start.21 = (f32[432,128]{1,0:T(8,128)S(1)}, f32[432,128]{1,0:T(8,128)S(1)}, u32[]{:S(2)}, u32[]{:S(2)}) collective-permute-start(f32[432,128]{1,0:T(8,128)S(1)} %fusion.refs_1_), channel_id=1, source_target_pairs={{0,4},{1,5},{2,6},{3,7},{4,0},{5,1},{6,2},{7,3},{8,12},{9,13},{10,... | collective-permute-start | bytes 663560 | tf_op jit(solution)/shard_map/ppermute | solution.py:293
  68.7 7.4 %collective-permute-start.20 = (f32[48,1024]{1,0:T(8,128)S(1)}, f32[48,1024]{1,0:T(8,128)S(1)}, u32[]{:S(2)}, u32[]{:S(2)}) collective-permute-start(f32[48,1024]{1,0:T(8,128)S(1)} %add.55), channel_id=1, source_target_pairs={{0,16},{8,24},{16,0},{24,8},{1,17},{9,25},{17,1},{25,9},{2,18},{10... | collective-permute-start | bytes 589832 | tf_op jit(solution)/shard_map/ppermute | solution.py:293
  71.2 10.2 %collective-permute-start.15 = (f32[144,128]{1,0:T(8,128)S(1)}, f32[144,128]{1,0:T(8,128)S(1)}, u32[]{:S(2)}, u32[]{:S(2)}) collective-permute-start(f32[144,128]{1,0:T(8,128)S(1)} %bitcast_add_fusion), channel_id=1, source_target_pairs={{0,16},{8,24},{16,0},{24,8},{1,17},{9,25},{17,1},{25,9},{2,18},{10... | collective-permute-start | bytes 221192 | tf_op jit(solution)/shard_map/ppermute | solution.py:293
  78.1 11.2 %collective-permute-start.22 = (f32[432,128]{1,0:T(8,128)S(1)}, f32[432,128]{1,0:T(8,128)S(1)}, u32[]{:S(2)}, u32[]{:S(2)}) collective-permute-start(f32[432,128]{1,0:T(8,128)S(1)} %add.67), channel_id=1, source_target_pairs={{0,2},{1,3},{2,0},{3,1},{4,6},{5,7},{6,4},{7,5},{8,10},{9,11},{10,... | collective-permute-start | bytes 663560 | tf_op jit(solution)/shard_map/ppermute | solution.py:293
  81.5 3.6 %collective-permute-start.16 = (f32[144,128]{1,0:T(8,128)S(1)}, f32[144,128]{1,0:T(8,128)S(1)}, u32[]{:S(2)}, u32[]{:S(2)}) collective-permute-start(f32[144,128]{1,0:T(8,128)S(1)} %add.63), channel_id=1, source_target_pairs={{0,1},{1,0},{2,3},{3,2},{4,5},{5,4},{6,7},{7,6},{8,9},{9,8},{10,11... | collective-permute-start | bytes 221192 | tf_op jit(solution)/shard_map/ppermute | solution.py:293
  85.1 3.3 %collective-permute-start.17 = (f32[144,128]{1,0:T(8,128)S(1)}, f32[144,128]{1,0:T(8,128)S(1)}, u32[]{:S(2)}, u32[]{:S(2)}) collective-permute-start(f32[144,128]{1,0:T(8,128)S(1)} %add.64), channel_id=1, source_target_pairs={{0,2},{1,3},{2,0},{3,1},{4,6},{5,7},{6,4},{7,5},{8,10},{9,11},{10,... | collective-permute-start | bytes 221192 | tf_op jit(solution)/shard_map/ppermute | solution.py:293
  88.3 5.1 %collective-permute-start.18 = (f32[144,128]{1,0:T(8,128)S(1)}, f32[144,128]{1,0:T(8,128)S(1)}, u32[]{:S(2)}, u32[]{:S(2)}) collective-permute-start(f32[144,128]{1,0:T(8,128)S(1)} %add.65), channel_id=1, source_target_pairs={{0,4},{1,5},{2,6},{3,7},{4,0},{5,1},{6,2},{7,3},{8,12},{9,13},{10,... | collective-permute-start | bytes 221192 | tf_op jit(solution)/shard_map/ppermute | solution.py:293
  89.4 14.0 %collective-permute-start.23 = (f32[864,128]{1,0:T(8,128)S(1)}, f32[864,128]{1,0:T(8,128)S(1)}, u32[]{:S(2)}, u32[]{:S(2)}) collective-permute-start(f32[864,128]{1,0:T(8,128)S(1)} %constant_dynamic-update-slice_fusion.refs_0_), channel_id=1, source_target_pairs={{0,16},{1,17},{10,26},{11,27},{20,4},{21,5},{30,14},{31,15}} | collective-permute-start | bytes 1327112 | tf_op jit(solution)/shard_map/ppermute | solution.py:427
  93.5 5.4 %collective-permute-start.19 = (f32[144,128]{1,0:T(8,128)S(1)}, f32[144,128]{1,0:T(8,128)S(1)}, u32[]{:S(2)}, u32[]{:S(2)}) collective-permute-start(f32[144,128]{1,0:T(8,128)S(1)} %add.66), channel_id=1, source_target_pairs={{0,8},{8,0},{16,24},{24,16},{1,9},{9,1},{17,25},{25,17},{2,10},{10... | collective-permute-start | bytes 221192 | tf_op jit(solution)/shard_map/ppermute | solution.py:293
  96.5 14.3 %collective-permute-start.24 = (f32[432,128]{1,0:T(8,128)S(1)}, f32[432,128]{1,0:T(8,128)S(1)}, u32[]{:S(2)}, u32[]{:S(2)}) collective-permute-start(f32[432,128]{1,0:T(8,128)S(1)} %add.67), channel_id=1, source_target_pairs={{0,4},{1,5},{2,6},{3,7},{4,0},{5,1},{6,2},{7,3},{8,12},{9,13},{10,... | collective-permute-start | bytes 663560 | tf_op jit(solution)/shard_map/ppermute | solution.py:293
  96.5 21.4 %collective-permute-start.25 = (f32[432,128]{1,0:T(8,128)S(1)}, f32[432,128]{1,0:T(8,128)S(1)}, u32[]{:S(2)}, u32[]{:S(2)}) collective-permute-start(f32[432,128]{1,0:T(8,128)S(1)} %add.67), channel_id=1, source_target_pairs={{0,6},{1,7},{2,4},{3,5},{4,2},{5,3},{6,0},{7,1},{8,14},{9,15},{10,... | collective-permute-start | bytes 663560 | tf_op jit(solution)/shard_map/ppermute | solution.py:293
  98.3 23.0 %collective-permute-start.31 = (f32[96,1024]{1,0:T(8,128)S(1)}, f32[96,1024]{1,0:T(8,128)S(1)}, u32[]{:S(2)}, u32[]{:S(2)}) collective-permute-start(f32[96,1024]{1,0:T(8,128)S(1)} %pad_maximum_fusion), channel_id=1, source_target_pairs={{0,8},{8,0},{16,24},{24,16},{1,9},{9,1},{17,25},{25,17},{2,10},{10... | collective-permute-start | bytes 1179656 | tf_op jit(solution)/shard_map/ppermute | solution.py:293
  118.0 8.4 %collective-permute-start.27 = (f32[864,128]{1,0:T(8,128)S(1)}, f32[864,128]{1,0:T(8,128)S(1)}, u32[]{:S(2)}, u32[]{:S(2)}) collective-permute-start(f32[864,128]{1,0:T(8,128)S(1)} %constant_dynamic-update-slice_fusion.2.refs_1_), channel_id=1, source_target_pairs={{0,16},{1,17},{10,26},{11,27},{20,4},{21,5},{30,14},{31,15}} | collective-permute-start | bytes 1327112 | tf_op jit(solution)/shard_map/ppermute | solution.py:427
  121.2 14.6 %collective-permute-start.29 = (f32[864,128]{1,0:T(8,128)S(1)}, f32[864,128]{1,0:T(8,128)S(1)}, u32[]{:S(2)}, u32[]{:S(2)}) collective-permute-start(f32[864,128]{1,0:T(8,128)S(1)} %constant_dynamic-update-slice_fusion.refs_0_), channel_id=1, source_target_pairs={{0,1},{1,0},{2,3},{3,2},{4,5},{5,4},{6,7},{7,6},{8,9},{9,8},{10,11... | collective-permute-start | bytes 1327112 | tf_op jit(solution)/shard_map/ppermute | solution.py:293
  121.3 11.1 %collective-permute-start.26 = (f32[864,128]{1,0:T(8,128)S(1)}, f32[864,128]{1,0:T(8,128)S(1)}, u32[]{:S(2)}, u32[]{:S(2)}) collective-permute-start(f32[864,128]{1,0:T(8,128)S(1)} %broadcast_select_fusion.3), channel_id=1, source_target_pairs={{0,8},{16,24},{1,9},{17,25},{10,2},{26,18},{11,3},{27,19},{4,12},{... | collective-permute-start | bytes 1327112 | tf_op jit(solution)/shard_map/ppermute | solution.py:427
  126.4 6.1 %collective-permute-start.28 = (f32[864,128]{1,0:T(8,128)S(1)}, f32[864,128]{1,0:T(8,128)S(1)}, u32[]{:S(2)}, u32[]{:S(2)}) collective-permute-start(f32[864,128]{1,0:T(8,128)S(1)} %broadcast_select_fusion.2), channel_id=1, source_target_pairs={{0,8},{16,24},{1,9},{17,25},{10,2},{26,18},{11,3},{27,19},{4,12},{... | collective-permute-start | bytes 1327112 | tf_op jit(solution)/shard_map/ppermute | solution.py:427
  128.1 13.4 %collective-permute-start.30 = (f32[864,128]{1,0:T(8,128)S(1)}, f32[864,128]{1,0:T(8,128)S(1)}, u32[]{:S(2)}, u32[]{:S(2)}) collective-permute-start(f32[864,128]{1,0:T(8,128)S(1)} %constant_dynamic-update-slice_fusion.2.refs_1_), channel_id=1, source_target_pairs={{0,1},{1,0},{2,3},{3,2},{4,5},{5,4},{6,7},{7,6},{8,9},{9,8},{10,11... | collective-permute-start | bytes 1327112 | tf_op jit(solution)/shard_map/ppermute | solution.py:293
where the time goes:
time: 149 us
  waiting for transfers between devices  62.1 us (42%)
  starting transfers between devices  44.1 us (30%)
  Pallas kernels  37.1 us (25%)
  local copies, waits for them, and re-layouts  3.44 us (2%)
    ppermute x27, waiting for transfers between devices, swap(): return lax.ppermute(a, axis, [(i, i ^ mask) for i in range(n)])  58.3 us
    ppermute x27, starting transfers between devices, swap(): return lax.ppermute(a, axis, [(i, i ^ mask) for i in range(n)])  33.3 us
    pallas_call x3, Pallas kernels, eliminated(): pl.pallas_call(functools.partial(inverse_kernel, first, last), out_shape=...  12.8 us
    pallas_call x4, Pallas kernels, row_terms(): pl.pallas_call(functools.partial(terms_kernel, n, streams, e, tuple(group...  11 us
    ppermute x4, starting transfers between devices, handed(): return jnp.where(handed_to[mask], lax.ppermute(a, ('row', 'col'), pairs), a)  10.1 us
    pallas_call x1, Pallas kernels, updated(): pl.pallas_call(functools.partial(update_kernel, n), out_shape=jax.ShapeDt...  7.53 us
    ppermute x4, waiting for transfers between devices, handed(): return jnp.where(handed_to[mask], lax.ppermute(a, ('row', 'col'), pairs), a)  3.73 us
    unnamed x13, local copies, waits for them, and re-layouts  3.38 us
  transfers between devices with their start and end apart: 32, of which 16 were waited for; matrix products, arithmetic and copies ran while one was open for 1% of the time, Pallas kernels for 19%

commit v1 on v0

--- a/solution.py
+++ b/solution.py
@@ -355,44 +355,40 @@
         transposed = [
             (z_ * nc + k * r_ + x_, r_ * nc + k * z_ + x_) for r_ in range(nr) for z_ in range(nr) for x_ in range(k)
         ]
-        made, kept = [], []
-        predicted, placed, first_of, handed_to = lax.optimization_barrier((predicted, placed, first_of, handed_to))
-        made.append(terms_of(1, groups[0], placed))
+        x_piece = lax.ppermute(xt, ("row", "col"), transposed)
         predicted, placed = step_on(predicted, placed)
-        predicted = after(predicted, made[0])
-        x_piece = lax.ppermute(after(xt, made[0]), ("row", "col"), transposed)
-        made.append(terms_of(1, groups[1], placed))
-        predicted, placed = step_on(predicted, placed)
-        predicted = after(predicted, made[1])
-        kept.append(terms_of(0, groups[0], placed))
-        predicted, placed, x_piece = step_on(predicted, placed, x_piece)
-        predicted = after(predicted, kept[0])
-        kept.append(terms_of(0, groups[1], placed))
+        placed, first_of, handed_to = lax.optimization_barrier((placed, first_of, handed_to))
+        made = [terms_of(1, group, placed) for group in groups]
         sent = []
         for a in made:
             sent.append(swap(a, "col", 1))
-        while len(sends) > 1:
-            predicted, sent[0], kept[1] = step_on(predicted, sent[0], kept[1])
-        x_far = swap(after(x_piece, kept[1]), "col", masks[-1] * k)
-        predicted, sent[1] = lax.optimization_barrier((predicted, sent[1]))
+        kept = [terms_of(0, group, placed) for group in groups]
+        predicted = after(predicted, made[0])
+        while sends[0][0] == "row":
+            (predicted,) = step_on(predicted)
+        predicted, kept[1], x_piece = lax.optimization_barrier((predicted, kept[1], x_piece))
+        while len(sends) > 2:
+            (predicted,) = step_on(predicted)
+        predicted, sent[0] = lax.optimization_barrier((predicted, sent[0]))
 
         part = {}
         for group, a, b in zip(groups, kept, sent):
             for i, d in enumerate(group):
                 part[d] = a[i * size : (i + 1) * size] + b[i * size : (i + 1) * size]
-        for mask in masks[:-1]:
+        for mask in masks:
             for d in sorted(part, reverse=True):
                 if d & mask:
                     got = swap(part.pop(d), "col", mask * k)
                     part[d ^ mask] = part[d ^ mask] + got
-        last = masks[-1]
-        predicted, part[0] = step_on(predicted, part[0])
-        got = swap(part[last], "col", last * k)
+        while len(sends) > 1:
+            (predicted,) = step_on(predicted)
+        (predicted,) = step_on(predicted)
+        predicted, u_piece = lax.optimization_barrier((predicted, part[0]))
 
         if fits:
-            inner = inner_of([part[0], part[last]], [x_piece, x_far], piece, batch)
+            inner = inner_of([u_piece], [x_piece], piece, batch)
         else:
-            inner = (dot(part[0], x_piece, (0, 0)) + dot(part[last], x_far, (0, 0))).reshape(2, batch // 2, batch)
+            inner = dot(u_piece, x_piece, (0, 0)).reshape(2, batch // 2, batch)
         low = first_of[1]
         inner = jnp.where(low, inner[0], inner[1]) + swap(jnp.where(low, inner[1], inner[0]), "row", 1)
         for mask in masks[1:]:
@@ -400,16 +396,14 @@
         for mask in bits_of(k):
             hop = swap(inner, "col", mask)
             inner = inner + hop
-        u_piece = part[0] + got
-        for mask in reversed(masks):
-            predicted = jnp.concatenate(ordered(first_of[mask], predicted, swap(predicted, "row", mask)))
-            if mask > 1:
-                predicted, u_piece = lax.optimization_barrier((predicted, u_piece))
         for mask in masks:
             inner = inner + swap(inner, "col", mask * k)
         inner = jnp.stack(ordered(low, inner, swap(inner, "row", 1)))
         if not fits:
             inner = inner.reshape(batch, batch)
+        for mask in reversed(masks):
+            got = swap(predicted, "row", mask)
+            predicted = jnp.concatenate(ordered(first_of[mask], predicted, got))
 
         u_by = {0: u_piece}
         for d in range(1, nr):

time: 149 us -> 138 us (0.926)
  the two profiles are of different devices: /device:TPU:11 before, /device:TPU:0 now
where the time goes in v1:
time: 138 us
  waiting for transfers between devices  57 us (41%)
  starting transfers between devices  39.2 us (28%)
  Pallas kernels  36.1 us (26%)
  local copies, waits for them, and re-layouts  3.43 us (2%)
    ppermute x26, waiting for transfers between devices, swap(): return lax.ppermute(a, axis, [(i, i ^ mask) for i in range(n)])  54.2 us
    ppermute x26, starting transfers between devices, swap(): return lax.ppermute(a, axis, [(i, i ^ mask) for i in range(n)])  29.6 us
    pallas_call x3, Pallas kernels, eliminated(): pl.pallas_call(functools.partial(inverse_kernel, first, last), out_shape=...  12.8 us
    pallas_call x4, Pallas kernels, row_terms(): pl.pallas_call(functools.partial(terms_kernel, n, streams, e, tuple(group...  10.4 us
    ppermute x4, starting transfers between devices, handed(): return jnp.where(handed_to[mask], lax.ppermute(a, ('row', 'col'), pairs), a)  8.93 us
    pallas_call x1, Pallas kernels, updated(): pl.pallas_call(functools.partial(update_kernel, n), out_shape=jax.ShapeDt...  7.53 us
    unnamed x13, local copies, waits for them, and re-layouts  3.37 us
  transfers between devices with their start and end apart: 31, of which 14 were waited for; matrix products, arithmetic and copies ran while one was open for 2% of the time, Pallas kernels for 16%

profile of v1, /device:TPU:0, one launch (start us, length us, event | category | flops | bytes accessed | tf_op | source)
XLA Modules:
  0.0 138.1 jit_solution(1714856970197268682)
XLA Ops:
  0.6 1.3 copy-done.1
  1.9 1.0 copy-done.3
  2.9 0.8 product.2
  4.3 1.1 copy.6
  5.5 2.6 %collective-permute-start.2 = (f32[432,128]{1,0:T(8,128)S(1)}, f32[432,128]{1,0:T(8,128)S(1)}, u32[]{:S(2)}, u32[]{:S(2)}) collective-permute-start(f32[432,128]{1,0:T(8,128)S(1)} %maximum_maximum_fusion.refs_0_), channel_id=1, source_target_pairs={{0,16},{8,24},{16,0},{24,8},{1,17},{9,25},{17,1},{25,9},{2,18},{10... | collective-permute-start | bytes 663560 | tf_op jit(solution)/shard_map/ppermute | solution.py:293
  8.4 5.8 %collective-permute-done.2.refs_2_ = f32[432,128]{1,0:T(8,128)S(1)} collective-permute-done((f32[432,128]{1,0:T(8,128)S(1)}, f32[432,128]{1,0:T(8,128)S(1)}, u32[]{:S(2)}, u32[]{:S(2)}) %collective-permute-start.2) | collective-permute-done | bytes 221216 | tf_op jit(solution)/shard_map/ppermute | solution.py:293
  14.3 1.4 collective-permute-done.3.refs_3_
  15.7 0.7 place.1
  16.4 4.6 %terms.4 = f32[864,128]{1,0:T(8,128)S(1)} custom-call(s32[3]{0:T(128)S(1)} %pad_add_fusion.place, f32[2304,1152]{1,0:T(8,128)} %cov_ref.9, bf16[4,288,192]{2,1,0:T(8,128)(2,1)S(1)} %get-tuple-element.31.high_ref, bf16[4,288,192]{2,1,0:T(8,128)(2,1)S(1)} %get-tuple-element.32.low_ref), custom_call_target="tpu_custom_call" | custom-call | flops 764411904 | bytes 2654208 | tf_op jit(solution)/shard_map/terms/pallas_call | solution.py:194
  21.0 1.8 %collective-permute-start.4 = (f32[48,1024]{1,0:T(8,128)S(1)}, f32[48,1024]{1,0:T(8,128)S(1)}, u32[]{:S(2)}, u32[]{:S(2)}) collective-permute-start(f32[48,1024]{1,0:T(8,128)S(1)} %slice_select_fusion.1), channel_id=1, source_target_pairs={{0,16},{8,24},{16,0},{24,8},{1,17},{9,25},{17,1},{25,9},{2,18},{10... | collective-permute-start | bytes 589832 | tf_op jit(solution)/shard_map/ppermute | solution.py:293
  22.8 0.7 collective-permute-start.5
  23.5 1.6 %collective-permute-start.7 = (f32[864,128]{1,0:T(8,128)S(1)}, f32[864,128]{1,0:T(8,128)S(1)}, u32[]{:S(2)}, u32[]{:S(2)}) collective-permute-start(f32[864,128]{1,0:T(8,128)S(1)} %terms.4), channel_id=1, source_target_pairs={{0,1},{1,0},{2,3},{3,2},{4,5},{5,4},{6,7},{7,6},{8,9},{9,8},{10,11... | collective-permute-start | bytes 1327112 | tf_op jit(solution)/shard_map/ppermute | solution.py:293
  25.1 1.9 %terms.5 = f32[864,128]{1,0:T(8,128)S(1)} custom-call(s32[3]{0:T(128)S(1)} %pad_add_fusion.place, f32[2304,1152]{1,0:T(8,128)S(1)} %copy-done, bf16[4,288,192]{2,1,0:T(8,128)(2,1)S(1)} %get-tuple-element.31.high_ref, bf16[4,288,192]{2,1,0:T(8,128)(2,1)S(1)} %get-tuple-element.32.low_ref), custom_call_target="tpu_custom_call" | custom-call | flops 764411904 | bytes 2654208 | tf_op jit(solution)/shard_map/terms/pallas_call | solution.py:194
  27.0 1.9 %terms.6 = f32[864,128]{1,0:T(8,128)S(1)} custom-call(s32[3]{0:T(128)S(1)} %pad_add_fusion.place, f32[2304,1152]{1,0:T(8,128)S(1)} %copy-done, bf16[4,288,192]{2,1,0:T(8,128)(2,1)S(1)} %get-tuple-element.31.high_ref, bf16[4,288,192]{2,1,0:T(8,128)(2,1)S(1)} %get-tuple-element.32.low_ref), custom_call_target="tpu_custom_call" | custom-call | flops 764411904 | bytes 2654208 | tf_op jit(solution)/shard_map/terms/pallas_call | solution.py:194
  29.6 2.9 %collective-permute-start.6 = (f32[48,1024]{1,0:T(8,128)S(1)}, f32[48,1024]{1,0:T(8,128)S(1)}, u32[]{:S(2)}, u32[]{:S(2)}) collective-permute-start(f32[48,1024]{1,0:T(8,128)S(1)} %select_add_fusion.1), channel_id=1, source_target_pairs={{0,2},{1,3},{2,0},{3,1},{4,6},{5,7},{6,4},{7,5},{8,10},{9,11},{10,... | collective-permute-start | bytes 589832 | tf_op jit(solution)/shard_map/ppermute | solution.py:293
  32.5 1.9 %terms.7 = f32[864,128]{1,0:T(8,128)S(1)} custom-call(s32[3]{0:T(128)S(1)} %pad_add_fusion.place, f32[2304,1152]{1,0:T(8,128)S(1)} %copy-done, bf16[4,288,192]{2,1,0:T(8,128)(2,1)S(1)} %get-tuple-element.31.high_ref, bf16[4,288,192]{2,1,0:T(8,128)(2,1)S(1)} %get-tuple-element.32.low_ref), custom_call_target="tpu_custom_call" | custom-call | flops 764411904 | bytes 2654208 | tf_op jit(solution)/shard_map/terms/pallas_call | solution.py:194
  34.4 5.7 %collective-permute-done.6 = f32[48,1024]{1,0:T(8,128)S(1)} collective-permute-done((f32[48,1024]{1,0:T(8,128)S(1)}, f32[48,1024]{1,0:T(8,128)S(1)}, u32[]{:S(2)}, u32[]{:S(2)}) %collective-permute-start.6) | collective-permute-done | bytes 196640 | tf_op jit(solution)/shard_map/ppermute | solution.py:293
  40.1 3.8 %collective-permute-start.8 = (f32[48,1024]{1,0:T(8,128)S(1)}, f32[48,1024]{1,0:T(8,128)S(1)}, u32[]{:S(2)}, u32[]{:S(2)}) collective-permute-start(f32[48,1024]{1,0:T(8,128)S(1)} %add.53), channel_id=1, source_target_pairs={{0,4},{1,5},{2,6},{3,7},{4,0},{5,1},{6,2},{7,3},{8,12},{9,13},{10,... | collective-permute-start | bytes 589832 | tf_op jit(solution)/shard_map/ppermute | solution.py:293
  44.0 1.1 collective-permute-start.12
  45.1 1.5 %collective-permute-start.11 = (f32[432,128]{1,0:T(8,128)S(1)}, f32[432,128]{1,0:T(8,128)S(1)}, u32[]{:S(2)}, u32[]{:S(2)}) collective-permute-start(f32[432,128]{1,0:T(8,128)S(1)} %slice_add_fusion.2), channel_id=1, source_target_pairs={{0,2},{1,3},{2,0},{3,1},{4,6},{5,7},{6,4},{7,5},{8,10},{9,11},{10,... | collective-permute-start | bytes 663560 | tf_op jit(solution)/shard_map/ppermute | solution.py:293
  46.6 8.9 %collective-permute-done.12 = f32[432,128]{1,0:T(8,128)S(1)} collective-permute-done((f32[432,128]{1,0:T(8,128)S(1)}, f32[432,128]{1,0:T(8,128)S(1)}, u32[]{:S(2)}, u32[]{:S(2)}) %collective-permute-start.12) | collective-permute-done | bytes 221216 | tf_op jit(solution)/shard_map/ppermute | solution.py:293
  55.7 1.7 %collective-permute-start.9 = (f32[48,1024]{1,0:T(8,128)S(1)}, f32[48,1024]{1,0:T(8,128)S(1)}, u32[]{:S(2)}, u32[]{:S(2)}) collective-permute-start(f32[48,1024]{1,0:T(8,128)S(1)} %add.54), channel_id=1, source_target_pairs={{0,1},{1,0},{2,3},{3,2},{4,5},{5,4},{6,7},{7,6},{8,9},{9,8},{10,11... | collective-permute-start | bytes 589832 | tf_op jit(solution)/shard_map/ppermute | solution.py:293
  57.4 5.9 %collective-permute-done.9 = f32[48,1024]{1,0:T(8,128)S(1)} collective-permute-done((f32[48,1024]{1,0:T(8,128)S(1)}, f32[48,1024]{1,0:T(8,128)S(1)}, u32[]{:S(2)}, u32[]{:S(2)}) %collective-permute-start.9) | collective-permute-done | bytes 196640 | tf_op jit(solution)/shard_map/ppermute | solution.py:293
  63.4 5.9 %collective-permute-done.13 = f32[432,128]{1,0:T(8,128)S(1)} collective-permute-done((f32[432,128]{1,0:T(8,128)S(1)}, f32[432,128]{1,0:T(8,128)S(1)}, u32[]{:S(2)}, u32[]{:S(2)}) %collective-permute-start.13) | collective-permute-done | bytes 221216 | tf_op jit(solution)/shard_map/ppermute | solution.py:293
  69.3 0.7 inner.1
  70.2 1.1 collective-permute-done.14
  71.3 0.9 collective-permute-start.15
  72.8 3.9 %collective-permute-start.23 = (f32[432,128]{1,0:T(8,128)S(1)}, f32[432,128]{1,0:T(8,128)S(1)}, u32[]{:S(2)}, u32[]{:S(2)}) collective-permute-start(f32[432,128]{1,0:T(8,128)S(1)} %fusion.2.refs_0_), channel_id=1, source_target_pairs={{0,6},{1,7},{2,4},{3,5},{4,2},{5,3},{6,0},{7,1},{8,14},{9,15},{10,... | collective-permute-start | bytes 663560 | tf_op jit(solution)/shard_map/ppermute | solution.py:293
  76.7 2.3 %collective-permute-done.15 = f32[144,128]{1,0:T(8,128)S(1)} collective-permute-done((f32[144,128]{1,0:T(8,128)S(1)}, f32[144,128]{1,0:T(8,128)S(1)}, u32[]{:S(2)}, u32[]{:S(2)}) %collective-permute-start.15) | collective-permute-done | bytes 73760 | tf_op jit(solution)/shard_map/ppermute | solution.py:293
  79.0 1.6 %collective-permute-start.16 = (f32[144,128]{1,0:T(8,128)S(1)}, f32[144,128]{1,0:T(8,128)S(1)}, u32[]{:S(2)}, u32[]{:S(2)}) collective-permute-start(f32[144,128]{1,0:T(8,128)S(1)} %add.64), channel_id=1, source_target_pairs={{0,1},{1,0},{2,3},{3,2},{4,5},{5,4},{6,7},{7,6},{8,9},{9,8},{10,11... | collective-permute-start | bytes 221192 | tf_op jit(solution)/shard_map/ppermute | solution.py:293
  80.6 2.8 %collective-permute-done.16 = f32[144,128]{1,0:T(8,128)S(1)} collective-permute-done((f32[144,128]{1,0:T(8,128)S(1)}, f32[144,128]{1,0:T(8,128)S(1)}, u32[]{:S(2)}, u32[]{:S(2)}) %collective-permute-start.16) | collective-permute-done | bytes 73760 | tf_op jit(solution)/shard_map/ppermute | solution.py:293
  83.5 7.9 %collective-permute-done.17 = f32[144,128]{1,0:T(8,128)S(1)} collective-permute-done((f32[144,128]{1,0:T(8,128)S(1)}, f32[144,128]{1,0:T(8,128)S(1)}, u32[]{:S(2)}, u32[]{:S(2)}) %collective-permute-start.17) | collective-permute-done | bytes 73760 | tf_op jit(solution)/shard_map/ppermute | solution.py:293
  91.6 3.0 %collective-permute-start.21 = (f32[864,128]{1,0:T(8,128)S(1)}, f32[864,128]{1,0:T(8,128)S(1)}, u32[]{:S(2)}, u32[]{:S(2)}) collective-permute-start(f32[864,128]{1,0:T(8,128)S(1)} %constant_dynamic-update-slice_fusion.refs_0_), channel_id=1, source_target_pairs={{0,16},{1,17},{10,26},{11,27},{20,4},{21,5},{30,14},{31,15}} | collective-permute-start | bytes 1327112 | tf_op jit(solution)/shard_map/ppermute | solution.py:421
  94.6 3.2 %collective-permute-done.18 = f32[144,128]{1,0:T(8,128)S(1)} collective-permute-done((f32[144,128]{1,0:T(8,128)S(1)}, f32[144,128]{1,0:T(8,128)S(1)}, u32[]{:S(2)}, u32[]{:S(2)}) %collective-permute-start.18) | collective-permute-done | bytes 73760 | tf_op jit(solution)/shard_map/ppermute | solution.py:293
  98.5 0.7 collective-permute-done.19
  99.2 4.4 %inverse.3.s_ref = f32[192,256]{1,0:T(8,128)S(1)} custom-call(f32[2,144,128]{2,1,0:T(8,128)S(1)} %pad_maximum_fusion.1.s_ref), custom_call_target="tpu_custom_call" | custom-call | flops 14155776 | bytes 294912 | tf_op jit(solution)/shard_map/inverse/pallas_call | solution.py:101
  103.7 4.2 %inverse.4.s_ref = f32[192,256]{1,0:T(8,128)S(1)} custom-call(f32[192,256]{1,0:T(8,128)S(1)} %inverse.3.s_ref), custom_call_target="tpu_custom_call" | custom-call | flops 14155776 | bytes 294912 | tf_op jit(solution)/shard_map/inverse/pallas_call | solution.py:101
  107.9 3.1 %collective-permute-start.25 = (f32[864,128]{1,0:T(8,128)S(1)}, f32[864,128]{1,0:T(8,128)S(1)}, u32[]{:S(2)}, u32[]{:S(2)}) collective-permute-start(f32[864,128]{1,0:T(8,128)S(1)} %constant_dynamic-update-slice_fusion.2.refs_1_), channel_id=1, source_target_pairs={{0,16},{1,17},{10,26},{11,27},{20,4},{21,5},{30,14},{31,15}} | collective-permute-start | bytes 1327112 | tf_op jit(solution)/shard_map/ppermute | solution.py:421
  111.1 1.6 %collective-permute-start.27 = (f32[864,128]{1,0:T(8,128)S(1)}, f32[864,128]{1,0:T(8,128)S(1)}, u32[]{:S(2)}, u32[]{:S(2)}) collective-permute-start(f32[864,128]{1,0:T(8,128)S(1)} %constant_dynamic-update-slice_fusion.refs_0_), channel_id=1, source_target_pairs={{0,1},{1,0},{2,3},{3,2},{4,5},{5,4},{6,7},{7,6},{8,9},{9,8},{10,11... | collective-permute-start | bytes 1327112 | tf_op jit(solution)/shard_map/ppermute | solution.py:293
  112.8 1.3 collective-permute-start.24
  114.1 2.7 %collective-permute-done.25 = f32[864,128]{1,0:T(8,128)S(1)} collective-permute-done((f32[864,128]{1,0:T(8,128)S(1)}, f32[864,128]{1,0:T(8,128)S(1)}, u32[]{:S(2)}, u32[]{:S(2)}) %collective-permute-start.25) | collective-permute-done | bytes 442400 | tf_op jit(solution)/shard_map/ppermute | solution.py:421
  116.9 1.5 %collective-permute-start.26 = (f32[864,128]{1,0:T(8,128)S(1)}, f32[864,128]{1,0:T(8,128)S(1)}, u32[]{:S(2)}, u32[]{:S(2)}) collective-permute-start(f32[864,128]{1,0:T(8,128)S(1)} %broadcast_select_fusion.2), channel_id=1, source_target_pairs={{0,8},{16,24},{1,9},{17,25},{10,2},{26,18},{11,3},{27,19},{4,12},{... | collective-permute-start | bytes 1327112 | tf_op jit(solution)/shard_map/ppermute | solution.py:421
  118.6 1.6 %collective-permute-start.28 = (f32[864,128]{1,0:T(8,128)S(1)}, f32[864,128]{1,0:T(8,128)S(1)}, u32[]{:S(2)}, u32[]{:S(2)}) collective-permute-start(f32[864,128]{1,0:T(8,128)S(1)} %constant_dynamic-update-slice_fusion.2.refs_1_), channel_id=1, source_target_pairs={{0,1},{1,0},{2,3},{3,2},{4,5},{5,4},{6,7},{7,6},{8,9},{9,8},{10,11... | collective-permute-start | bytes 1327112 | tf_op jit(solution)/shard_map/ppermute | solution.py:293
  120.2 4.3 %inverse.5.inverse_ref = f32[192,256]{1,0:T(8,128)S(1)} custom-call(f32[192,256]{1,0:T(8,128)S(1)} %inverse.4.s_ref), custom_call_target="tpu_custom_call" | custom-call | flops 14155776 | bytes 294912 | tf_op jit(solution)/shard_map/inverse/pallas_call | solution.py:101
  124.6 1.5 %gain.1 = (bf16[192,1152]{1,0:T(8,128)(2,1)S(1)}, bf16[192,1152]{1,0:T(8,128)(2,1)S(1)}, f32[288,192]{1,0:T(8,128)S(1)}) custom-call(s32[3]{0:T(128)S(1)} %pad_add_fusion.place, f32[192,256]{1,0:T(8,128)S(1)} %inverse.5.inverse_ref, f32[864,128]{1,0:T(8,128)S(1)} %broadcast_select_fusion.1.refs_0_, f32[864,128]{1,0:T(8,128)S(1)} %broadcast_select_fusion.refs_1_), custom_call_target="tpu_custom_call" | custom-call | tf_op jit(solution)/shard_map/gain/pallas_call | solution.py:232
  126.2 1.7 %product.3 = f32[288,1024]{1,0:T(8,128)} custom-call(f32[288,192]{1,0:T(8,128)S(1)} %get-tuple-element.49.a_ref, f32[192,1024]{1,0:T(8,128)S(1)} %maximum_subtract_fusion.b_ref, f32[288,1024]{1,0:T(8,128)S(1)} %copy-done.2), custom_call_target="tpu_custom_call" | custom-call | tf_op jit(solution)/shard_map/product/pallas_call | solution.py:142
  127.8 2.6 %collective-permute-done.28.refs_3_ = f32[864,128]{1,0:T(8,128)S(1)} collective-permute-done((f32[864,128]{1,0:T(8,128)S(1)}, f32[864,128]{1,0:T(8,128)S(1)}, u32[]{:S(2)}, u32[]{:S(2)}) %collective-permute-start.28) | collective-permute-done | bytes 442400 | tf_op jit(solution)/shard_map/ppermute | solution.py:293
  130.4 7.5 %update.1 = f32[2304,1152]{1,0:T(8,128)} custom-call(s32[3]{0:T(128)S(1)} %pad_add_fusion.place, f32[2304,1152]{1,0:T(8,128)S(1)} %copy-done, bf16[192,1152]{1,0:T(8,128)(2,1)S(1)} %get-tuple-element.47.high_ref, bf16[192,1152]{1,0:T(8,128)(2,1)S(1)} %get-tuple-element.48.low_ref, f32[864,128]{1,0:T(8,128)S(1)} %constant_dynamic-update-slice_fusion.refs_0_, ...), custom_call_target="tpu_custom_call" | custom-call | tf_op jit(solution)/shard_map/update/pallas_call | solution.py:268
  (73 shorter events, 4.2 us)
Async XLA Ops:
  0.6 1.3 copy-start.1
  1.9 1.0 copy-start.3
  3.7 10.5 %collective-permute-start = (f32[96,1024]{1,0:T(8,128)S(1)}, f32[96,1024]{1,0:T(8,128)S(1)}, u32[]{:S(2)}, u32[]{:S(2)}) collective-permute-start(f32[96,1024]{1,0:T(8,128)S(1)} %slice_select_fusion), channel_id=1, source_target_pairs={{0,8},{8,0},{16,24},{24,16},{1,9},{9,1},{17,25},{25,17},{2,10},{10... | collective-permute-start | bytes 1179656 | tf_op jit(solution)/shard_map/ppermute | solution.py:293
  5.5 8.7 %collective-permute-start.2 = (f32[432,128]{1,0:T(8,128)S(1)}, f32[432,128]{1,0:T(8,128)S(1)}, u32[]{:S(2)}, u32[]{:S(2)}) collective-permute-start(f32[432,128]{1,0:T(8,128)S(1)} %maximum_maximum_fusion.refs_0_), channel_id=1, source_target_pairs={{0,16},{8,24},{16,0},{24,8},{1,17},{9,25},{17,1},{25,9},{2,18},{10... | collective-permute-start | bytes 663560 | tf_op jit(solution)/shard_map/ppermute | solution.py:293
  8.1 6.2 %collective-permute-start.1 = (f32[432,128]{1,0:T(8,128)S(1)}, f32[432,128]{1,0:T(8,128)S(1)}, u32[]{:S(2)}, u32[]{:S(2)}) collective-permute-start(f32[432,128]{1,0:T(8,128)S(1)} %maximum_maximum_fusion.refs_0_), channel_id=1, source_target_pairs={{0,8},{8,0},{16,24},{24,16},{1,9},{9,1},{17,25},{25,17},{2,10},{10... | collective-permute-start | bytes 663560 | tf_op jit(solution)/shard_map/ppermute | solution.py:293
  8.3 16.7 %copy-start = (f32[2304,1152]{1,0:T(8,128)S(1)}, f32[2304,1152]{1,0:T(8,128)}, u32[]{:S(2)}) copy-start(f32[2304,1152]{1,0:T(8,128)} %cov_ref.9) | copy-start | bytes 31850500
  14.2 1.5 %collective-permute-start.3 = (f32[432,128]{1,0:T(8,128)S(1)}, f32[432,128]{1,0:T(8,128)S(1)}, u32[]{:S(2)}, u32[]{:S(2)}) collective-permute-start(f32[432,128]{1,0:T(8,128)S(1)} %collective-permute-done.2.refs_2_), channel_id=1, source_target_pairs={{0,8},{8,0},{16,24},{24,16},{1,9},{9,1},{17,25},{25,17},{2,10},{10... | collective-permute-start | bytes 663560 | tf_op jit(solution)/shard_map/ppermute | solution.py:293
  21.0 8.5 %collective-permute-start.4 = (f32[48,1024]{1,0:T(8,128)S(1)}, f32[48,1024]{1,0:T(8,128)S(1)}, u32[]{:S(2)}, u32[]{:S(2)}) collective-permute-start(f32[48,1024]{1,0:T(8,128)S(1)} %slice_select_fusion.1), channel_id=1, source_target_pairs={{0,16},{8,24},{16,0},{24,8},{1,17},{9,25},{17,1},{25,9},{2,18},{10... | collective-permute-start | bytes 589832 | tf_op jit(solution)/shard_map/ppermute | solution.py:293
  22.8 6.8 %collective-permute-start.5 = (f32[432,128]{1,0:T(8,128)S(1)}, f32[432,128]{1,0:T(8,128)S(1)}, u32[]{:S(2)}, u32[]{:S(2)}) collective-permute-start(f32[432,128]{1,0:T(8,128)S(1)} %maximum_maximum_fusion.refs_0_), channel_id=1, source_target_pairs={{0,0},{1,1},{8,2},{9,3},{16,4},{17,5},{24,6},{25,7},{2,8},{3,9},{1... | collective-permute-start | bytes 663560 | tf_op jit(solution)/shard_map/ppermute | solution.py:358
  23.5 16.6 %collective-permute-start.7 = (f32[864,128]{1,0:T(8,128)S(1)}, f32[864,128]{1,0:T(8,128)S(1)}, u32[]{:S(2)}, u32[]{:S(2)}) collective-permute-start(f32[864,128]{1,0:T(8,128)S(1)} %terms.4), channel_id=1, source_target_pairs={{0,1},{1,0},{2,3},{3,2},{4,5},{5,4},{6,7},{7,6},{8,9},{9,8},{10,11... | collective-permute-start | bytes 1327112 | tf_op jit(solution)/shard_map/ppermute | solution.py:293
  28.9 16.2 %collective-permute-start.10 = (f32[864,128]{1,0:T(8,128)S(1)}, f32[864,128]{1,0:T(8,128)S(1)}, u32[]{:S(2)}, u32[]{:S(2)}) collective-permute-start(f32[864,128]{1,0:T(8,128)S(1)} %terms.6), channel_id=1, source_target_pairs={{0,1},{1,0},{2,3},{3,2},{4,5},{5,4},{6,7},{7,6},{8,9},{9,8},{10,11... | collective-permute-start | bytes 1327112 | tf_op jit(solution)/shard_map/ppermute | solution.py:293
  29.6 10.5 %collective-permute-start.6 = (f32[48,1024]{1,0:T(8,128)S(1)}, f32[48,1024]{1,0:T(8,128)S(1)}, u32[]{:S(2)}, u32[]{:S(2)}) collective-permute-start(f32[48,1024]{1,0:T(8,128)S(1)} %select_add_fusion.1), channel_id=1, source_target_pairs={{0,2},{1,3},{2,0},{3,1},{4,6},{5,7},{6,4},{7,5},{8,10},{9,11},{10,... | collective-permute-start | bytes 589832 | tf_op jit(solution)/shard_map/ppermute | solution.py:293
  34.4 84.0 %copy-start.4 = (s32[192]{0:T(256)S(1)}, s32[192]{0:T(256)}, u32[]{:S(2)}) copy-start(s32[192]{0:T(256)} %param.6) | copy-start | bytes 2308
  40.1 86.0 %copy-start.2 = (f32[288,1024]{1,0:T(8,128)S(1)}, f32[288,1024]{1,0:T(8,128)}, u32[]{:S(2)}) copy-start(f32[288,1024]{1,0:T(8,128)} %c_ref.1) | copy-start | bytes 3538948
  40.1 15.5 %collective-permute-start.8 = (f32[48,1024]{1,0:T(8,128)S(1)}, f32[48,1024]{1,0:T(8,128)S(1)}, u32[]{:S(2)}, u32[]{:S(2)}) collective-permute-start(f32[48,1024]{1,0:T(8,128)S(1)} %add.53), channel_id=1, source_target_pairs={{0,4},{1,5},{2,6},{3,7},{4,0},{5,1},{6,2},{7,3},{8,12},{9,13},{10,... | collective-permute-start | bytes 589832 | tf_op jit(solution)/shard_map/ppermute | solution.py:293
  44.0 11.5 %collective-permute-start.12 = (f32[432,128]{1,0:T(8,128)S(1)}, f32[432,128]{1,0:T(8,128)S(1)}, u32[]{:S(2)}, u32[]{:S(2)}) collective-permute-start(f32[432,128]{1,0:T(8,128)S(1)} %slice_add_fusion), channel_id=1, source_target_pairs={{0,2},{1,3},{2,0},{3,1},{4,6},{5,7},{6,4},{7,5},{8,10},{9,11},{10,... | collective-permute-start | bytes 663560 | tf_op jit(solution)/shard_map/ppermute | solution.py:293
  45.1 18.2 %collective-permute-start.11 = (f32[432,128]{1,0:T(8,128)S(1)}, f32[432,128]{1,0:T(8,128)S(1)}, u32[]{:S(2)}, u32[]{:S(2)}) collective-permute-start(f32[432,128]{1,0:T(8,128)S(1)} %slice_add_fusion.2), channel_id=1, source_target_pairs={{0,2},{1,3},{2,0},{3,1},{4,6},{5,7},{6,4},{7,5},{8,10},{9,11},{10,... | collective-permute-start | bytes 663560 | tf_op jit(solution)/shard_map/ppermute | solution.py:293
  55.6 13.7 %collective-permute-start.13 = (f32[432,128]{1,0:T(8,128)S(1)}, f32[432,128]{1,0:T(8,128)S(1)}, u32[]{:S(2)}, u32[]{:S(2)}) collective-permute-start(f32[432,128]{1,0:T(8,128)S(1)} %fusion), channel_id=1, source_target_pairs={{0,4},{1,5},{2,6},{3,7},{4,0},{5,1},{6,2},{7,3},{8,12},{9,13},{10,... | collective-permute-start | bytes 663560 | tf_op jit(solution)/shard_map/ppermute | solution.py:293
  55.7 7.7 %collective-permute-start.9 = (f32[48,1024]{1,0:T(8,128)S(1)}, f32[48,1024]{1,0:T(8,128)S(1)}, u32[]{:S(2)}, u32[]{:S(2)}) collective-permute-start(f32[48,1024]{1,0:T(8,128)S(1)} %add.54), channel_id=1, source_target_pairs={{0,1},{1,0},{2,3},{3,2},{4,5},{5,4},{6,7},{7,6},{8,9},{9,8},{10,11... | collective-permute-start | bytes 589832 | tf_op jit(solution)/shard_map/ppermute | solution.py:293
  70.0 1.3 collective-permute-start.14
  70.2 13.3 %collective-permute-start.29 = (f32[48,1024]{1,0:T(8,128)S(1)}, f32[48,1024]{1,0:T(8,128)S(1)}, u32[]{:S(2)}, u32[]{:S(2)}) collective-permute-start(f32[48,1024]{1,0:T(8,128)S(1)} %add.55), channel_id=1, source_target_pairs={{0,16},{8,24},{16,0},{24,8},{1,17},{9,25},{17,1},{25,9},{2,18},{10... | collective-permute-start | bytes 589832 | tf_op jit(solution)/shard_map/ppermute | solution.py:293
  71.3 7.6 %collective-permute-start.15 = (f32[144,128]{1,0:T(8,128)S(1)}, f32[144,128]{1,0:T(8,128)S(1)}, u32[]{:S(2)}, u32[]{:S(2)}) collective-permute-start(f32[144,128]{1,0:T(8,128)S(1)} %bitcast_add_fusion), channel_id=1, source_target_pairs={{0,16},{8,24},{16,0},{24,8},{1,17},{9,25},{17,1},{25,9},{2,18},{10... | collective-permute-start | bytes 221192 | tf_op jit(solution)/shard_map/ppermute | solution.py:293
  72.3 19.3 %collective-permute-start.20 = (f32[432,128]{1,0:T(8,128)S(1)}, f32[432,128]{1,0:T(8,128)S(1)}, u32[]{:S(2)}, u32[]{:S(2)}) collective-permute-start(f32[432,128]{1,0:T(8,128)S(1)} %fusion.2.refs_0_), channel_id=1, source_target_pairs={{0,2},{1,3},{2,0},{3,1},{4,6},{5,7},{6,4},{7,5},{8,10},{9,11},{10,... | collective-permute-start | bytes 663560 | tf_op jit(solution)/shard_map/ppermute | solution.py:293
  72.3 35.6 %collective-permute-start.22 = (f32[432,128]{1,0:T(8,128)S(1)}, f32[432,128]{1,0:T(8,128)S(1)}, u32[]{:S(2)}, u32[]{:S(2)}) collective-permute-start(f32[432,128]{1,0:T(8,128)S(1)} %fusion.2.refs_0_), channel_id=1, source_target_pairs={{0,4},{1,5},{2,6},{3,7},{4,0},{5,1},{6,2},{7,3},{8,12},{9,13},{10,... | collective-permute-start | bytes 663560 | tf_op jit(solution)/shard_map/ppermute | solution.py:293
  72.8 35.1 %collective-permute-start.23 = (f32[432,128]{1,0:T(8,128)S(1)}, f32[432,128]{1,0:T(8,128)S(1)}, u32[]{:S(2)}, u32[]{:S(2)}) collective-permute-start(f32[432,128]{1,0:T(8,128)S(1)} %fusion.2.refs_0_), channel_id=1, source_target_pairs={{0,6},{1,7},{2,4},{3,5},{4,2},{5,3},{6,0},{7,1},{8,14},{9,15},{10,... | collective-permute-start | bytes 663560 | tf_op jit(solution)/shard_map/ppermute | solution.py:293
  79.0 4.4 %collective-permute-start.16 = (f32[144,128]{1,0:T(8,128)S(1)}, f32[144,128]{1,0:T(8,128)S(1)}, u32[]{:S(2)}, u32[]{:S(2)}) collective-permute-start(f32[144,128]{1,0:T(8,128)S(1)} %add.64), channel_id=1, source_target_pairs={{0,1},{1,0},{2,3},{3,2},{4,5},{5,4},{6,7},{7,6},{8,9},{9,8},{10,11... | collective-permute-start | bytes 221192 | tf_op jit(solution)/shard_map/ppermute | solution.py:293
  83.4 8.1 %collective-permute-start.17 = (f32[144,128]{1,0:T(8,128)S(1)}, f32[144,128]{1,0:T(8,128)S(1)}, u32[]{:S(2)}, u32[]{:S(2)}) collective-permute-start(f32[144,128]{1,0:T(8,128)S(1)} %add.65), channel_id=1, source_target_pairs={{0,2},{1,3},{2,0},{3,1},{4,6},{5,7},{6,4},{7,5},{8,10},{9,11},{10,... | collective-permute-start | bytes 221192 | tf_op jit(solution)/shard_map/ppermute | solution.py:293
  91.5 6.3 %collective-permute-start.18 = (f32[144,128]{1,0:T(8,128)S(1)}, f32[144,128]{1,0:T(8,128)S(1)}, u32[]{:S(2)}, u32[]{:S(2)}) collective-permute-start(f32[144,128]{1,0:T(8,128)S(1)} %add.66), channel_id=1, source_target_pairs={{0,4},{1,5},{2,6},{3,7},{4,0},{5,1},{6,2},{7,3},{8,12},{9,13},{10,... | collective-permute-start | bytes 221192 | tf_op jit(solution)/shard_map/ppermute | solution.py:293
  91.6 12.0 %collective-permute-start.21 = (f32[864,128]{1,0:T(8,128)S(1)}, f32[864,128]{1,0:T(8,128)S(1)}, u32[]{:S(2)}, u32[]{:S(2)}) collective-permute-start(f32[864,128]{1,0:T(8,128)S(1)} %constant_dynamic-update-slice_fusion.refs_0_), channel_id=1, source_target_pairs={{0,16},{1,17},{10,26},{11,27},{20,4},{21,5},{30,14},{31,15}} | collective-permute-start | bytes 1327112 | tf_op jit(solution)/shard_map/ppermute | solution.py:421
  97.8 1.3 collective-permute-start.19
  97.9 14.8 %collective-permute-start.30 = (f32[96,1024]{1,0:T(8,128)S(1)}, f32[96,1024]{1,0:T(8,128)S(1)}, u32[]{:S(2)}, u32[]{:S(2)}) collective-permute-start(f32[96,1024]{1,0:T(8,128)S(1)} %pad_maximum_fusion), channel_id=1, source_target_pairs={{0,8},{8,0},{16,24},{24,16},{1,9},{9,1},{17,25},{25,17},{2,10},{10... | collective-permute-start | bytes 1179656 | tf_op jit(solution)/shard_map/ppermute | solution.py:293
  107.9 8.9 %collective-permute-start.25 = (f32[864,128]{1,0:T(8,128)S(1)}, f32[864,128]{1,0:T(8,128)S(1)}, u32[]{:S(2)}, u32[]{:S(2)}) collective-permute-start(f32[864,128]{1,0:T(8,128)S(1)} %constant_dynamic-update-slice_fusion.2.refs_1_), channel_id=1, source_target_pairs={{0,16},{1,17},{10,26},{11,27},{20,4},{21,5},{30,14},{31,15}} | collective-permute-start | bytes 1327112 | tf_op jit(solution)/shard_map/ppermute | solution.py:421
  111.1 16.7 %collective-permute-start.27 = (f32[864,128]{1,0:T(8,128)S(1)}, f32[864,128]{1,0:T(8,128)S(1)}, u32[]{:S(2)}, u32[]{:S(2)}) collective-permute-start(f32[864,128]{1,0:T(8,128)S(1)} %constant_dynamic-update-slice_fusion.refs_0_), channel_id=1, source_target_pairs={{0,1},{1,0},{2,3},{3,2},{4,5},{5,4},{6,7},{7,6},{8,9},{9,8},{10,11... | collective-permute-start | bytes 1327112 | tf_op jit(solution)/shard_map/ppermute | solution.py:293
  112.8 11.7 %collective-permute-start.24 = (f32[864,128]{1,0:T(8,128)S(1)}, f32[864,128]{1,0:T(8,128)S(1)}, u32[]{:S(2)}, u32[]{:S(2)}) collective-permute-start(f32[864,128]{1,0:T(8,128)S(1)} %broadcast_select_fusion.3), channel_id=1, source_target_pairs={{0,8},{16,24},{1,9},{17,25},{10,2},{26,18},{11,3},{27,19},{4,12},{... | collective-permute-start | bytes 1327112 | tf_op jit(solution)/shard_map/ppermute | solution.py:421
  116.9 7.6 %collective-permute-start.26 = (f32[864,128]{1,0:T(8,128)S(1)}, f32[864,128]{1,0:T(8,128)S(1)}, u32[]{:S(2)}, u32[]{:S(2)}) collective-permute-start(f32[864,128]{1,0:T(8,128)S(1)} %broadcast_select_fusion.2), channel_id=1, source_target_pairs={{0,8},{16,24},{1,9},{17,25},{10,2},{26,18},{11,3},{27,19},{4,12},{... | collective-permute-start | bytes 1327112 | tf_op jit(solution)/shard_map/ppermute | solution.py:421
  118.6 11.8 %collective-permute-start.28 = (f32[864,128]{1,0:T(8,128)S(1)}, f32[864,128]{1,0:T(8,128)S(1)}, u32[]{:S(2)}, u32[]{:S(2)}) collective-permute-start(f32[864,128]{1,0:T(8,128)S(1)} %constant_dynamic-update-slice_fusion.2.refs_1_), channel_id=1, source_target_pairs={{0,1},{1,0},{2,3},{3,2},{4,5},{5,4},{6,7},{7,6},{8,9},{9,8},{10,11... | collective-permute-start | bytes 1327112 | tf_op jit(solution)/shard_map/ppermute | solution.py:293

commit v2 on v1

--- a/solution.py
+++ b/solution.py
@@ -336,14 +336,13 @@
                 return jnp.concatenate([lax.dynamic_slice_in_dim(whole, i, piece, 0) for i in at])
 
         predicted = product(samples, weights) if fits else dot(samples, weights, (1, 0))
-        sends = [("row", row, m, True) for m in masks] + [("col", z, m * k, False) for m in masks]
-        sends += [("col", x, 1, False)]
+        sends = [("row", 1)] + [("col", m * k) for m in masks] + [("row", m) for m in masks[1:]] + [("col", 1)]
 
         def step_on(predicted, *others):
-            axis, index, mask, halves_it = sends.pop(0)
-            if halves_it:
+            axis, mask = sends.pop(0)
+            if (axis, mask) == ("row", 1):
                 n = predicted.shape[0] // 2
-                low = (index & mask) == 0
+                low = first_of[mask]
                 a, b = predicted[:n], predicted[n:]
                 keep, give = jnp.where(low, a, b), jnp.where(low, b, a)
             else:
@@ -356,20 +355,18 @@
             (z_ * nc + k * r_ + x_, r_ * nc + k * z_ + x_) for r_ in range(nr) for z_ in range(nr) for x_ in range(k)
         ]
         x_piece = lax.ppermute(xt, ("row", "col"), transposed)
-        predicted, placed = step_on(predicted, placed)
+        (predicted,) = step_on(predicted)
         placed, first_of, handed_to = lax.optimization_barrier((placed, first_of, handed_to))
-        made = [terms_of(1, group, placed) for group in groups]
-        sent = []
-        for a in made:
-            sent.append(swap(a, "col", 1))
-        kept = [terms_of(0, group, placed) for group in groups]
-        predicted = after(predicted, made[0])
-        while sends[0][0] == "row":
+        made, sent, kept = [], [], []
+        for i, group in enumerate(groups):
+            made.append(terms_of(1, group, placed))
+            sent.append(swap(made[i], "col", 1))
+        for group in groups:
+            kept.append(terms_of(0, group, placed))
+        while sends[1][0] == "col":
             (predicted,) = step_on(predicted)
-        predicted, kept[1], x_piece = lax.optimization_barrier((predicted, kept[1], x_piece))
-        while len(sends) > 2:
-            (predicted,) = step_on(predicted)
-        predicted, sent[0] = lax.optimization_barrier((predicted, sent[0]))
+            predicted = after(predicted, made[1])
+        (predicted,) = step_on(predicted)
 
         part = {}
         for group, a, b in zip(groups, kept, sent):
@@ -380,10 +377,8 @@
                 if d & mask:
                     got = swap(part.pop(d), "col", mask * k)
                     part[d ^ mask] = part[d ^ mask] + got
-        while len(sends) > 1:
-            (predicted,) = step_on(predicted)
-        (predicted,) = step_on(predicted)
-        predicted, u_piece = lax.optimization_barrier((predicted, part[0]))
+        u_piece = part[0]
+        x_piece = after(x_piece, kept[1])
 
         if fits:
             inner = inner_of([u_piece], [x_piece], piece, batch)
@@ -391,19 +386,22 @@
             inner = dot(u_piece, x_piece, (0, 0)).reshape(2, batch // 2, batch)
         low = first_of[1]
         inner = jnp.where(low, inner[0], inner[1]) + swap(jnp.where(low, inner[1], inner[0]), "row", 1)
+        for mask in reversed(masks):
+            hop = swap(inner, "col", mask * k)
+            inner = inner + hop
+            if mask == masks[-1]:
+                u_piece = after(u_piece, inner)
+        while sends:
+            (predicted,) = step_on(predicted)
         for mask in masks[1:]:
             inner = inner + swap(inner, "row", mask)
         for mask in bits_of(k):
-            hop = swap(inner, "col", mask)
-            inner = inner + hop
-        for mask in masks:
-            inner = inner + swap(inner, "col", mask * k)
+            inner = inner + swap(inner, "col", mask)
         inner = jnp.stack(ordered(low, inner, swap(inner, "row", 1)))
         if not fits:
             inner = inner.reshape(batch, batch)
-        for mask in reversed(masks):
-            got = swap(predicted, "row", mask)
-            predicted = jnp.concatenate(ordered(first_of[mask], predicted, got))
+        got = swap(predicted, "row", 1)
+        predicted = jnp.concatenate(ordered(first_of[1], predicted, got))
 
         u_by = {0: u_piece}
         for d in range(1, nr):

time: 138 us -> 147 us (1.065)
  the two profiles are of different devices: /device:TPU:0 before, /device:TPU:9 now
where the time goes in v2:
time: 147 us; the launch traced here: 146 us
  starting transfers between devices  52 us (35%)
  waiting for transfers between devices  51.9 us (35%)
  Pallas kernels  36.8 us (25%)
  local copies, waits for them, and re-layouts  3.43 us (2%)
    ppermute x25, waiting for transfers between devices, swap(): return lax.ppermute(a, axis, [(i, i ^ mask) for i in range(n)])  51 us
    ppermute x25, starting transfers between devices, swap(): return lax.ppermute(a, axis, [(i, i ^ mask) for i in range(n)])  41.7 us
    pallas_call x3, Pallas kernels, eliminated(): pl.pallas_call(functools.partial(inverse_kernel, first, last), out_shape=...  12.9 us
    pallas_call x4, Pallas kernels, row_terms(): pl.pallas_call(functools.partial(terms_kernel, n, streams, e, tuple(group...  11.1 us
    ppermute x4, starting transfers between devices, handed(): return jnp.where(handed_to[mask], lax.ppermute(a, ('row', 'col'), pairs), a)  9.59 us
    pallas_call x1, Pallas kernels, updated(): pl.pallas_call(functools.partial(update_kernel, n), out_shape=jax.ShapeDt...  7.53 us
    unnamed x13, local copies, waits for them, and re-layouts  3.38 us
  transfers between devices with their start and end apart: 30, of which 15 were waited for; matrix products, arithmetic and copies ran while one was open for 1% of the time, Pallas kernels for 20%

profile of v2, /device:TPU:9, one launch (start us, length us, event | category | flops | bytes accessed | tf_op | source)
XLA Modules:
  0.0 146.5 jit_solution(892687584441567928)
XLA Ops:
  0.6 1.1 copy.6
  1.9 1.3 collective-permute-start.1
  3.2 1.3 copy-done.1
  4.4 1.0 copy-done.3
  6.3 1.0 collective-permute-start.24
  8.2 1.5 %collective-permute-start.2 = (f32[432,128]{1,0:T(8,128)S(1)}, f32[432,128]{1,0:T(8,128)S(1)}, u32[]{:S(2)}, u32[]{:S(2)}) collective-permute-start(f32[432,128]{1,0:T(8,128)S(1)} %collective-permute-done.1.refs_2_), channel_id=1, source_target_pairs={{0,8},{8,0},{16,24},{24,16},{1,9},{9,1},{17,25},{25,17},{2,10},{10... | collective-permute-start | bytes 663560 | tf_op jit(solution)/shard_map/ppermute | solution.py:293
  11.6 5.3 %terms.7 = f32[864,128]{1,0:T(8,128)S(1)} custom-call(s32[3]{0:T(128)S(1)} %pad_add_fusion.place, f32[2304,1152]{1,0:T(8,128)} %cov_ref.9, bf16[4,288,192]{2,1,0:T(8,128)(2,1)S(1)} %get-tuple-element.21.high_ref, bf16[4,288,192]{2,1,0:T(8,128)(2,1)S(1)} %get-tuple-element.22.low_ref), custom_call_target="tpu_custom_call" | custom-call | flops 764411904 | bytes 2654208 | tf_op jit(solution)/shard_map/terms/pallas_call | solution.py:194
  16.9 1.3 collective-permute-start.5
  18.2 1.9 %terms.5 = f32[864,128]{1,0:T(8,128)S(1)} custom-call(s32[3]{0:T(128)S(1)} %pad_add_fusion.place, f32[2304,1152]{1,0:T(8,128)S(1)} %copy-done, bf16[4,288,192]{2,1,0:T(8,128)(2,1)S(1)} %get-tuple-element.21.high_ref, bf16[4,288,192]{2,1,0:T(8,128)(2,1)S(1)} %get-tuple-element.22.low_ref), custom_call_target="tpu_custom_call" | custom-call | flops 764411904 | bytes 2654208 | tf_op jit(solution)/shard_map/terms/pallas_call | solution.py:194
  20.5 2.2 %collective-permute-start.25 = (f32[96,1024]{1,0:T(8,128)S(1)}, f32[96,1024]{1,0:T(8,128)S(1)}, u32[]{:S(2)}, u32[]{:S(2)}) collective-permute-start(f32[96,1024]{1,0:T(8,128)S(1)} %select_add_fusion), channel_id=1, source_target_pairs={{0,2},{1,3},{2,0},{3,1},{4,6},{5,7},{6,4},{7,5},{8,10},{9,11},{10,... | collective-permute-start | bytes 1179656 | tf_op jit(solution)/shard_map/ppermute | solution.py:293
  22.7 1.9 %terms.6 = f32[864,128]{1,0:T(8,128)S(1)} custom-call(s32[3]{0:T(128)S(1)} %pad_add_fusion.place, f32[2304,1152]{1,0:T(8,128)S(1)} %copy-done, bf16[4,288,192]{2,1,0:T(8,128)(2,1)S(1)} %get-tuple-element.21.high_ref, bf16[4,288,192]{2,1,0:T(8,128)(2,1)S(1)} %get-tuple-element.22.low_ref), custom_call_target="tpu_custom_call" | custom-call | flops 764411904 | bytes 2654208 | tf_op jit(solution)/shard_map/terms/pallas_call | solution.py:194
  24.6 1.9 %terms.4 = f32[864,128]{1,0:T(8,128)S(1)} custom-call(s32[3]{0:T(128)S(1)} %pad_add_fusion.place, f32[2304,1152]{1,0:T(8,128)S(1)} %copy-done, bf16[4,288,192]{2,1,0:T(8,128)(2,1)S(1)} %get-tuple-element.21.high_ref, bf16[4,288,192]{2,1,0:T(8,128)(2,1)S(1)} %get-tuple-element.22.low_ref), custom_call_target="tpu_custom_call" | custom-call | flops 764411904 | bytes 2654208 | tf_op jit(solution)/shard_map/terms/pallas_call | solution.py:194
  26.6 1.0 collective-permute-done.5
  27.6 3.8 %collective-permute-start.6 = (f32[432,128]{1,0:T(8,128)S(1)}, f32[432,128]{1,0:T(8,128)S(1)}, u32[]{:S(2)}, u32[]{:S(2)}) collective-permute-start(f32[432,128]{1,0:T(8,128)S(1)} %slice_add_fusion), channel_id=1, source_target_pairs={{0,2},{1,3},{2,0},{3,1},{4,6},{5,7},{6,4},{7,5},{8,10},{9,11},{10,... | collective-permute-start | bytes 663560 | tf_op jit(solution)/shard_map/ppermute | solution.py:293
  31.4 5.7 %collective-permute-done.3 = f32[864,128]{1,0:T(8,128)S(1)} collective-permute-done((f32[864,128]{1,0:T(8,128)S(1)}, f32[864,128]{1,0:T(8,128)S(1)}, u32[]{:S(2)}, u32[]{:S(2)}) %collective-permute-start.3) | collective-permute-done | bytes 442400 | tf_op jit(solution)/shard_map/ppermute | solution.py:293
  37.1 2.2 %collective-permute-start.4 = (f32[432,128]{1,0:T(8,128)S(1)}, f32[432,128]{1,0:T(8,128)S(1)}, u32[]{:S(2)}, u32[]{:S(2)}) collective-permute-start(f32[432,128]{1,0:T(8,128)S(1)} %slice_add_fusion.2), channel_id=1, source_target_pairs={{0,2},{1,3},{2,0},{3,1},{4,6},{5,7},{6,4},{7,5},{8,10},{9,11},{10,... | collective-permute-start | bytes 663560 | tf_op jit(solution)/shard_map/ppermute | solution.py:293
  39.3 3.1 %collective-permute-start.7 = (f32[432,128]{1,0:T(8,128)S(1)}, f32[432,128]{1,0:T(8,128)S(1)}, u32[]{:S(2)}, u32[]{:S(2)}) collective-permute-start(f32[432,128]{1,0:T(8,128)S(1)} %fusion), channel_id=1, source_target_pairs={{0,4},{1,5},{2,6},{3,7},{4,0},{5,1},{6,2},{7,3},{8,12},{9,13},{10,... | collective-permute-start | bytes 663560 | tf_op jit(solution)/shard_map/ppermute | solution.py:293
  42.5 6.0 %collective-permute-done.4 = f32[432,128]{1,0:T(8,128)S(1)} collective-permute-done((f32[432,128]{1,0:T(8,128)S(1)}, f32[432,128]{1,0:T(8,128)S(1)}, u32[]{:S(2)}, u32[]{:S(2)}) %collective-permute-start.4) | collective-permute-done | bytes 221216 | tf_op jit(solution)/shard_map/ppermute | solution.py:293
  48.5 11.0 %collective-permute-done.7 = f32[432,128]{1,0:T(8,128)S(1)} collective-permute-done((f32[432,128]{1,0:T(8,128)S(1)}, f32[432,128]{1,0:T(8,128)S(1)}, u32[]{:S(2)}, u32[]{:S(2)}) %collective-permute-start.7) | collective-permute-done | bytes 221216 | tf_op jit(solution)/shard_map/ppermute | solution.py:293
  60.3 3.0 %collective-permute-start.9 = (f32[144,128]{1,0:T(8,128)S(1)}, f32[144,128]{1,0:T(8,128)S(1)}, u32[]{:S(2)}, u32[]{:S(2)}) collective-permute-start(f32[144,128]{1,0:T(8,128)S(1)} %select_bitcast_fusion.2), channel_id=1, source_target_pairs={{0,8},{8,0},{16,24},{24,16},{1,9},{9,1},{17,25},{25,17},{2,10},{10... | collective-permute-start | bytes 221192 | tf_op jit(solution)/shard_map/ppermute | solution.py:293
  64.3 3.2 %collective-permute-start.10 = (f32[144,128]{1,0:T(8,128)S(1)}, f32[144,128]{1,0:T(8,128)S(1)}, u32[]{:S(2)}, u32[]{:S(2)}) collective-permute-start(f32[144,128]{1,0:T(8,128)S(1)} %bitcast_add_fusion), channel_id=1, source_target_pairs={{0,4},{1,5},{2,6},{3,7},{4,0},{5,1},{6,2},{7,3},{8,12},{9,13},{10,... | collective-permute-start | bytes 221192 | tf_op jit(solution)/shard_map/ppermute | solution.py:293
  67.4 2.1 %collective-permute-done.26 = f32[96,1024]{1,0:T(8,128)S(1)} collective-permute-done((f32[96,1024]{1,0:T(8,128)S(1)}, f32[96,1024]{1,0:T(8,128)S(1)}, u32[]{:S(2)}, u32[]{:S(2)}) %collective-permute-start.26) | collective-permute-done | bytes 393248 | tf_op jit(solution)/shard_map/ppermute | solution.py:293
  69.6 1.9 %collective-permute-start.27 = (f32[96,1024]{1,0:T(8,128)S(1)}, f32[96,1024]{1,0:T(8,128)S(1)}, u32[]{:S(2)}, u32[]{:S(2)}) collective-permute-start(f32[96,1024]{1,0:T(8,128)S(1)} %add.65), channel_id=1, source_target_pairs={{0,16},{8,24},{16,0},{24,8},{1,17},{9,25},{17,1},{25,9},{2,18},{10... | collective-permute-start | bytes 1179656 | tf_op jit(solution)/shard_map/ppermute | solution.py:293
  71.5 3.5 %collective-permute-start.15 = (f32[432,128]{1,0:T(8,128)S(1)}, f32[432,128]{1,0:T(8,128)S(1)}, u32[]{:S(2)}, u32[]{:S(2)}) collective-permute-start(f32[432,128]{1,0:T(8,128)S(1)} %fusion.2.refs_0_), channel_id=1, source_target_pairs={{0,2},{1,3},{2,0},{3,1},{4,6},{5,7},{6,4},{7,5},{8,10},{9,11},{10,... | collective-permute-start | bytes 663560 | tf_op jit(solution)/shard_map/ppermute | solution.py:293
  75.0 4.8 %collective-permute-done.11 = f32[144,128]{1,0:T(8,128)S(1)} collective-permute-done((f32[144,128]{1,0:T(8,128)S(1)}, f32[144,128]{1,0:T(8,128)S(1)}, u32[]{:S(2)}, u32[]{:S(2)}) %collective-permute-start.11) | collective-permute-done | bytes 73760 | tf_op jit(solution)/shard_map/ppermute | solution.py:293
  79.8 2.6 %collective-permute-start.12 = (f32[144,128]{1,0:T(8,128)S(1)}, f32[144,128]{1,0:T(8,128)S(1)}, u32[]{:S(2)}, u32[]{:S(2)}) collective-permute-start(f32[144,128]{1,0:T(8,128)S(1)} %add.60), channel_id=1, source_target_pairs={{0,16},{8,24},{16,0},{24,8},{1,17},{9,25},{17,1},{25,9},{2,18},{10... | collective-permute-start | bytes 221192 | tf_op jit(solution)/shard_map/ppermute | solution.py:293
  82.4 1.7 %collective-permute-done.12 = f32[144,128]{1,0:T(8,128)S(1)} collective-permute-done((f32[144,128]{1,0:T(8,128)S(1)}, f32[144,128]{1,0:T(8,128)S(1)}, u32[]{:S(2)}, u32[]{:S(2)}) %collective-permute-start.12) | collective-permute-done | bytes 73760 | tf_op jit(solution)/shard_map/ppermute | solution.py:293
  84.2 1.3 collective-permute-start.13
  85.5 3.4 %collective-permute-start.16 = (f32[864,128]{1,0:T(8,128)S(1)}, f32[864,128]{1,0:T(8,128)S(1)}, u32[]{:S(2)}, u32[]{:S(2)}) collective-permute-start(f32[864,128]{1,0:T(8,128)S(1)} %constant_dynamic-update-slice_fusion.refs_0_), channel_id=1, source_target_pairs={{0,16},{1,17},{10,26},{11,27},{20,4},{21,5},{30,14},{31,15}} | collective-permute-start | bytes 1327112 | tf_op jit(solution)/shard_map/ppermute | solution.py:419
  88.9 3.0 %collective-permute-start.14 = (f32[144,128]{1,0:T(8,128)S(1)}, f32[144,128]{1,0:T(8,128)S(1)}, u32[]{:S(2)}, u32[]{:S(2)}) collective-permute-start(f32[144,128]{1,0:T(8,128)S(1)} %add.62), channel_id=1, source_target_pairs={{0,8},{8,0},{16,24},{24,16},{1,9},{9,1},{17,25},{25,17},{2,10},{10... | collective-permute-start | bytes 221192 | tf_op jit(solution)/shard_map/ppermute | solution.py:293
  91.9 1.3 collective-permute-start.28
  93.2 1.3 collective-permute-start.17
  94.5 1.3 collective-permute-start.18
  95.9 4.4 %inverse.3.s_ref = f32[192,256]{1,0:T(8,128)S(1)} custom-call(f32[2,144,128]{2,1,0:T(8,128)S(1)} %pad_maximum_fusion.s_ref), custom_call_target="tpu_custom_call" | custom-call | flops 14155776 | bytes 294912 | tf_op jit(solution)/shard_map/inverse/pallas_call | solution.py:101
  100.3 2.4 %collective-permute-done.28 = f32[96,1024]{1,0:T(8,128)S(1)} collective-permute-done((f32[96,1024]{1,0:T(8,128)S(1)}, f32[96,1024]{1,0:T(8,128)S(1)}, u32[]{:S(2)}, u32[]{:S(2)}) %collective-permute-start.28) | collective-permute-done | bytes 393248 | tf_op jit(solution)/shard_map/ppermute | solution.py:293
  103.7 4.2 %inverse.4.s_ref = f32[192,256]{1,0:T(8,128)S(1)} custom-call(f32[192,256]{1,0:T(8,128)S(1)} %inverse.3.s_ref), custom_call_target="tpu_custom_call" | custom-call | flops 14155776 | bytes 294912 | tf_op jit(solution)/shard_map/inverse/pallas_call | solution.py:101
  107.9 1.1 collective-permute-done.17
  109.0 6.7 %collective-permute-done.18 = f32[432,128]{1,0:T(8,128)S(1)} collective-permute-done((f32[432,128]{1,0:T(8,128)S(1)}, f32[432,128]{1,0:T(8,128)S(1)}, u32[]{:S(2)}, u32[]{:S(2)}) %collective-permute-start.18) | collective-permute-done | bytes 221216 | tf_op jit(solution)/shard_map/ppermute | solution.py:293
  115.7 3.4 %collective-permute-start.20 = (f32[864,128]{1,0:T(8,128)S(1)}, f32[864,128]{1,0:T(8,128)S(1)}, u32[]{:S(2)}, u32[]{:S(2)}) collective-permute-start(f32[864,128]{1,0:T(8,128)S(1)} %constant_dynamic-update-slice_fusion.2.refs_1_), channel_id=1, source_target_pairs={{0,16},{1,17},{10,26},{11,27},{20,4},{21,5},{30,14},{31,15}} | collective-permute-start | bytes 1327112 | tf_op jit(solution)/shard_map/ppermute | solution.py:419
  119.5 1.2 collective-permute-start.23
  120.7 1.3 collective-permute-start.19
  122.0 4.3 %inverse.5.inverse_ref = f32[192,256]{1,0:T(8,128)S(1)} custom-call(f32[192,256]{1,0:T(8,128)S(1)} %inverse.4.s_ref), custom_call_target="tpu_custom_call" | custom-call | flops 14155776 | bytes 294912 | tf_op jit(solution)/shard_map/inverse/pallas_call | solution.py:101
  126.4 1.5 %collective-permute-start.21 = (f32[864,128]{1,0:T(8,128)S(1)}, f32[864,128]{1,0:T(8,128)S(1)}, u32[]{:S(2)}, u32[]{:S(2)}) collective-permute-start(f32[864,128]{1,0:T(8,128)S(1)} %broadcast_select_fusion.2), channel_id=1, source_target_pairs={{0,8},{16,24},{1,9},{17,25},{10,2},{26,18},{11,3},{27,19},{4,12},{... | collective-permute-start | bytes 1327112 | tf_op jit(solution)/shard_map/ppermute | solution.py:419
  128.1 1.0 collective-permute-done.21
  129.2 1.5 %gain.1 = (bf16[192,1152]{1,0:T(8,128)(2,1)S(1)}, bf16[192,1152]{1,0:T(8,128)(2,1)S(1)}, f32[288,192]{1,0:T(8,128)S(1)}) custom-call(s32[3]{0:T(128)S(1)} %pad_add_fusion.place, f32[192,256]{1,0:T(8,128)S(1)} %inverse.5.inverse_ref, f32[864,128]{1,0:T(8,128)S(1)} %broadcast_select_fusion.1.refs_0_, f32[864,128]{1,0:T(8,128)S(1)} %broadcast_select_fusion.refs_1_), custom_call_target="tpu_custom_call" | custom-call | tf_op jit(solution)/shard_map/gain/pallas_call | solution.py:232
  130.7 1.7 %product.3 = f32[288,1024]{1,0:T(8,128)} custom-call(f32[288,192]{1,0:T(8,128)S(1)} %get-tuple-element.34.a_ref, f32[192,1024]{1,0:T(8,128)S(1)} %maximum_subtract_fusion.b_ref, f32[288,1024]{1,0:T(8,128)S(1)} %copy-done.2), custom_call_target="tpu_custom_call" | custom-call | tf_op jit(solution)/shard_map/product/pallas_call | solution.py:142
  132.4 6.4 %collective-permute-done.23.refs_3_ = f32[864,128]{1,0:T(8,128)S(1)} collective-permute-done((f32[864,128]{1,0:T(8,128)S(1)}, f32[864,128]{1,0:T(8,128)S(1)}, u32[]{:S(2)}, u32[]{:S(2)}) %collective-permute-start.23) | collective-permute-done | bytes 442400 | tf_op jit(solution)/shard_map/ppermute | solution.py:293
  138.8 7.5 %update.1 = f32[2304,1152]{1,0:T(8,128)} custom-call(s32[3]{0:T(128)S(1)} %pad_add_fusion.place, f32[2304,1152]{1,0:T(8,128)S(1)} %copy-done, bf16[192,1152]{1,0:T(8,128)(2,1)S(1)} %get-tuple-element.32.high_ref, bf16[192,1152]{1,0:T(8,128)(2,1)S(1)} %get-tuple-element.33.low_ref, f32[864,128]{1,0:T(8,128)S(1)} %constant_dynamic-update-slice_fusion.refs_0_, ...), custom_call_target="tpu_custom_call" | custom-call | tf_op jit(solution)/shard_map/update/pallas_call | solution.py:268
  (68 shorter events, 8.1 us)
Async XLA Ops:
  1.9 6.4 %collective-permute-start.1 = (f32[432,128]{1,0:T(8,128)S(1)}, f32[432,128]{1,0:T(8,128)S(1)}, u32[]{:S(2)}, u32[]{:S(2)}) collective-permute-start(f32[432,128]{1,0:T(8,128)S(1)} %maximum_maximum_fusion.refs_0_), channel_id=1, source_target_pairs={{0,16},{8,24},{16,0},{24,8},{1,17},{9,25},{17,1},{25,9},{2,18},{10... | collective-permute-start | bytes 663560 | tf_op jit(solution)/shard_map/ppermute | solution.py:293
  3.2 1.3 copy-start.1
  4.4 1.0 copy-start.3
  6.3 14.2 %collective-permute-start.24 = (f32[96,1024]{1,0:T(8,128)S(1)}, f32[96,1024]{1,0:T(8,128)S(1)}, u32[]{:S(2)}, u32[]{:S(2)}) collective-permute-start(f32[96,1024]{1,0:T(8,128)S(1)} %slice_select_fusion), channel_id=1, source_target_pairs={{0,8},{8,0},{16,24},{24,16},{1,9},{9,1},{17,25},{25,17},{2,10},{10... | collective-permute-start | bytes 1179656 | tf_op jit(solution)/shard_map/ppermute | solution.py:293
  7.3 3.3 %collective-permute-start = (f32[432,128]{1,0:T(8,128)S(1)}, f32[432,128]{1,0:T(8,128)S(1)}, u32[]{:S(2)}, u32[]{:S(2)}) collective-permute-start(f32[432,128]{1,0:T(8,128)S(1)} %maximum_maximum_fusion.refs_0_), channel_id=1, source_target_pairs={{0,8},{8,0},{16,24},{24,16},{1,9},{9,1},{17,25},{25,17},{2,10},{10... | collective-permute-start | bytes 663560 | tf_op jit(solution)/shard_map/ppermute | solution.py:293
  8.2 2.6 %collective-permute-start.2 = (f32[432,128]{1,0:T(8,128)S(1)}, f32[432,128]{1,0:T(8,128)S(1)}, u32[]{:S(2)}, u32[]{:S(2)}) collective-permute-start(f32[432,128]{1,0:T(8,128)S(1)} %collective-permute-done.1.refs_2_), channel_id=1, source_target_pairs={{0,8},{8,0},{16,24},{24,16},{1,9},{9,1},{17,25},{25,17},{2,10},{10... | collective-permute-start | bytes 663560 | tf_op jit(solution)/shard_map/ppermute | solution.py:293
  9.8 32.6 %collective-permute-start.8 = (f32[432,128]{1,0:T(8,128)S(1)}, f32[432,128]{1,0:T(8,128)S(1)}, u32[]{:S(2)}, u32[]{:S(2)}) collective-permute-start(f32[432,128]{1,0:T(8,128)S(1)} %maximum_maximum_fusion.refs_0_), channel_id=1, source_target_pairs={{0,0},{1,1},{8,2},{9,3},{16,4},{17,5},{24,6},{25,7},{2,8},{3,9},{1... | collective-permute-start | bytes 663560 | tf_op jit(solution)/shard_map/ppermute | solution.py:357
  10.5 7.7 %copy-start = (f32[2304,1152]{1,0:T(8,128)S(1)}, f32[2304,1152]{1,0:T(8,128)}, u32[]{:S(2)}) copy-start(f32[2304,1152]{1,0:T(8,128)} %cov_ref.9) | copy-start | bytes 31850500
  16.9 10.7 %collective-permute-start.5 = (f32[864,128]{1,0:T(8,128)S(1)}, f32[864,128]{1,0:T(8,128)S(1)}, u32[]{:S(2)}, u32[]{:S(2)}) collective-permute-start(f32[864,128]{1,0:T(8,128)S(1)} %terms.7), channel_id=1, source_target_pairs={{0,1},{1,0},{2,3},{3,2},{4,5},{5,4},{6,7},{7,6},{8,9},{9,8},{10,11... | collective-permute-start | bytes 1327112 | tf_op jit(solution)/shard_map/ppermute | solution.py:293
  20.1 16.9 %collective-permute-start.3 = (f32[864,128]{1,0:T(8,128)S(1)}, f32[864,128]{1,0:T(8,128)S(1)}, u32[]{:S(2)}, u32[]{:S(2)}) collective-permute-start(f32[864,128]{1,0:T(8,128)S(1)} %terms.5), channel_id=1, source_target_pairs={{0,1},{1,0},{2,3},{3,2},{4,5},{5,4},{6,7},{7,6},{8,9},{9,8},{10,11... | collective-permute-start | bytes 1327112 | tf_op jit(solution)/shard_map/ppermute | solution.py:293
  20.5 21.9 %collective-permute-start.25 = (f32[96,1024]{1,0:T(8,128)S(1)}, f32[96,1024]{1,0:T(8,128)S(1)}, u32[]{:S(2)}, u32[]{:S(2)}) collective-permute-start(f32[96,1024]{1,0:T(8,128)S(1)} %select_add_fusion), channel_id=1, source_target_pairs={{0,2},{1,3},{2,0},{3,1},{4,6},{5,7},{6,4},{7,5},{8,10},{9,11},{10,... | collective-permute-start | bytes 1179656 | tf_op jit(solution)/shard_map/ppermute | solution.py:293
  26.6 101.3 %copy-start.4 = (s32[192]{0:T(256)S(1)}, s32[192]{0:T(256)}, u32[]{:S(2)}) copy-start(s32[192]{0:T(256)} %param.6) | copy-start | bytes 2308
  27.6 11.7 %collective-permute-start.6 = (f32[432,128]{1,0:T(8,128)S(1)}, f32[432,128]{1,0:T(8,128)S(1)}, u32[]{:S(2)}, u32[]{:S(2)}) collective-permute-start(f32[432,128]{1,0:T(8,128)S(1)} %slice_add_fusion), channel_id=1, source_target_pairs={{0,2},{1,3},{2,0},{3,1},{4,6},{5,7},{6,4},{7,5},{8,10},{9,11},{10,... | collective-permute-start | bytes 663560 | tf_op jit(solution)/shard_map/ppermute | solution.py:293
  37.1 11.5 %collective-permute-start.4 = (f32[432,128]{1,0:T(8,128)S(1)}, f32[432,128]{1,0:T(8,128)S(1)}, u32[]{:S(2)}, u32[]{:S(2)}) collective-permute-start(f32[432,128]{1,0:T(8,128)S(1)} %slice_add_fusion.2), channel_id=1, source_target_pairs={{0,2},{1,3},{2,0},{3,1},{4,6},{5,7},{6,4},{7,5},{8,10},{9,11},{10,... | collective-permute-start | bytes 663560 | tf_op jit(solution)/shard_map/ppermute | solution.py:293
  39.3 91.4 %copy-start.2 = (f32[288,1024]{1,0:T(8,128)S(1)}, f32[288,1024]{1,0:T(8,128)}, u32[]{:S(2)}) copy-start(f32[288,1024]{1,0:T(8,128)} %c_ref.1) | copy-start | bytes 3538948
  39.3 20.2 %collective-permute-start.7 = (f32[432,128]{1,0:T(8,128)S(1)}, f32[432,128]{1,0:T(8,128)S(1)}, u32[]{:S(2)}, u32[]{:S(2)}) collective-permute-start(f32[432,128]{1,0:T(8,128)S(1)} %fusion), channel_id=1, source_target_pairs={{0,4},{1,5},{2,6},{3,7},{4,0},{5,1},{6,2},{7,3},{8,12},{9,13},{10,... | collective-permute-start | bytes 663560 | tf_op jit(solution)/shard_map/ppermute | solution.py:293
  42.5 27.1 %collective-permute-start.26 = (f32[96,1024]{1,0:T(8,128)S(1)}, f32[96,1024]{1,0:T(8,128)S(1)}, u32[]{:S(2)}, u32[]{:S(2)}) collective-permute-start(f32[96,1024]{1,0:T(8,128)S(1)} %add.64), channel_id=1, source_target_pairs={{0,4},{1,5},{2,6},{3,7},{4,0},{5,1},{6,2},{7,3},{8,12},{9,13},{10,... | collective-permute-start | bytes 1179656 | tf_op jit(solution)/shard_map/ppermute | solution.py:293
  60.3 4.0 %collective-permute-start.9 = (f32[144,128]{1,0:T(8,128)S(1)}, f32[144,128]{1,0:T(8,128)S(1)}, u32[]{:S(2)}, u32[]{:S(2)}) collective-permute-start(f32[144,128]{1,0:T(8,128)S(1)} %select_bitcast_fusion.2), channel_id=1, source_target_pairs={{0,8},{8,0},{16,24},{24,16},{1,9},{9,1},{17,25},{25,17},{2,10},{10... | collective-permute-start | bytes 221192 | tf_op jit(solution)/shard_map/ppermute | solution.py:293
  64.3 7.2 %collective-permute-start.10 = (f32[144,128]{1,0:T(8,128)S(1)}, f32[144,128]{1,0:T(8,128)S(1)}, u32[]{:S(2)}, u32[]{:S(2)}) collective-permute-start(f32[144,128]{1,0:T(8,128)S(1)} %bitcast_add_fusion), channel_id=1, source_target_pairs={{0,4},{1,5},{2,6},{3,7},{4,0},{5,1},{6,2},{7,3},{8,12},{9,13},{10,... | collective-permute-start | bytes 221192 | tf_op jit(solution)/shard_map/ppermute | solution.py:293
  69.6 22.3 %collective-permute-start.27 = (f32[96,1024]{1,0:T(8,128)S(1)}, f32[96,1024]{1,0:T(8,128)S(1)}, u32[]{:S(2)}, u32[]{:S(2)}) collective-permute-start(f32[96,1024]{1,0:T(8,128)S(1)} %add.65), channel_id=1, source_target_pairs={{0,16},{8,24},{16,0},{24,8},{1,17},{9,25},{17,1},{25,9},{2,18},{10... | collective-permute-start | bytes 1179656 | tf_op jit(solution)/shard_map/ppermute | solution.py:293
  71.5 13.9 %collective-permute-start.15 = (f32[432,128]{1,0:T(8,128)S(1)}, f32[432,128]{1,0:T(8,128)S(1)}, u32[]{:S(2)}, u32[]{:S(2)}) collective-permute-start(f32[432,128]{1,0:T(8,128)S(1)} %fusion.2.refs_0_), channel_id=1, source_target_pairs={{0,2},{1,3},{2,0},{3,1},{4,6},{5,7},{6,4},{7,5},{8,10},{9,11},{10,... | collective-permute-start | bytes 663560 | tf_op jit(solution)/shard_map/ppermute | solution.py:293
  75.0 4.8 %collective-permute-start.11 = (f32[144,128]{1,0:T(8,128)S(1)}, f32[144,128]{1,0:T(8,128)S(1)}, u32[]{:S(2)}, u32[]{:S(2)}) collective-permute-start(f32[144,128]{1,0:T(8,128)S(1)} %add.59), channel_id=1, source_target_pairs={{0,2},{1,3},{2,0},{3,1},{4,6},{5,7},{6,4},{7,5},{8,10},{9,11},{10,... | collective-permute-start | bytes 221192 | tf_op jit(solution)/shard_map/ppermute | solution.py:293
  79.8 4.3 %collective-permute-start.12 = (f32[144,128]{1,0:T(8,128)S(1)}, f32[144,128]{1,0:T(8,128)S(1)}, u32[]{:S(2)}, u32[]{:S(2)}) collective-permute-start(f32[144,128]{1,0:T(8,128)S(1)} %add.60), channel_id=1, source_target_pairs={{0,16},{8,24},{16,0},{24,8},{1,17},{9,25},{17,1},{25,9},{2,18},{10... | collective-permute-start | bytes 221192 | tf_op jit(solution)/shard_map/ppermute | solution.py:293
  84.2 4.7 %collective-permute-start.13 = (f32[144,128]{1,0:T(8,128)S(1)}, f32[144,128]{1,0:T(8,128)S(1)}, u32[]{:S(2)}, u32[]{:S(2)}) collective-permute-start(f32[144,128]{1,0:T(8,128)S(1)} %add.61), channel_id=1, source_target_pairs={{0,1},{1,0},{2,3},{3,2},{4,5},{5,4},{6,7},{7,6},{8,9},{9,8},{10,11... | collective-permute-start | bytes 221192 | tf_op jit(solution)/shard_map/ppermute | solution.py:293
  85.5 18.2 %collective-permute-start.16 = (f32[864,128]{1,0:T(8,128)S(1)}, f32[864,128]{1,0:T(8,128)S(1)}, u32[]{:S(2)}, u32[]{:S(2)}) collective-permute-start(f32[864,128]{1,0:T(8,128)S(1)} %constant_dynamic-update-slice_fusion.refs_0_), channel_id=1, source_target_pairs={{0,16},{1,17},{10,26},{11,27},{20,4},{21,5},{30,14},{31,15}} | collective-permute-start | bytes 1327112 | tf_op jit(solution)/shard_map/ppermute | solution.py:419
  88.9 7.0 %collective-permute-start.14 = (f32[144,128]{1,0:T(8,128)S(1)}, f32[144,128]{1,0:T(8,128)S(1)}, u32[]{:S(2)}, u32[]{:S(2)}) collective-permute-start(f32[144,128]{1,0:T(8,128)S(1)} %add.62), channel_id=1, source_target_pairs={{0,8},{8,0},{16,24},{24,16},{1,9},{9,1},{17,25},{25,17},{2,10},{10... | collective-permute-start | bytes 221192 | tf_op jit(solution)/shard_map/ppermute | solution.py:293
  91.9 10.7 %collective-permute-start.28 = (f32[96,1024]{1,0:T(8,128)S(1)}, f32[96,1024]{1,0:T(8,128)S(1)}, u32[]{:S(2)}, u32[]{:S(2)}) collective-permute-start(f32[96,1024]{1,0:T(8,128)S(1)} %add.66), channel_id=1, source_target_pairs={{0,1},{1,0},{2,3},{3,2},{4,5},{5,4},{6,7},{7,6},{8,9},{9,8},{10,11... | collective-permute-start | bytes 1179656 | tf_op jit(solution)/shard_map/ppermute | solution.py:293
  93.2 15.8 %collective-permute-start.17 = (f32[432,128]{1,0:T(8,128)S(1)}, f32[432,128]{1,0:T(8,128)S(1)}, u32[]{:S(2)}, u32[]{:S(2)}) collective-permute-start(f32[432,128]{1,0:T(8,128)S(1)} %fusion.2.refs_0_), channel_id=1, source_target_pairs={{0,4},{1,5},{2,6},{3,7},{4,0},{5,1},{6,2},{7,3},{8,12},{9,13},{10,... | collective-permute-start | bytes 663560 | tf_op jit(solution)/shard_map/ppermute | solution.py:293
  94.5 21.2 %collective-permute-start.18 = (f32[432,128]{1,0:T(8,128)S(1)}, f32[432,128]{1,0:T(8,128)S(1)}, u32[]{:S(2)}, u32[]{:S(2)}) collective-permute-start(f32[432,128]{1,0:T(8,128)S(1)} %fusion.2.refs_0_), channel_id=1, source_target_pairs={{0,6},{1,7},{2,4},{3,5},{4,2},{5,3},{6,0},{7,1},{8,14},{9,15},{10,... | collective-permute-start | bytes 663560 | tf_op jit(solution)/shard_map/ppermute | solution.py:293
  102.7 23.6 %collective-permute-start.29 = (f32[96,1024]{1,0:T(8,128)S(1)}, f32[96,1024]{1,0:T(8,128)S(1)}, u32[]{:S(2)}, u32[]{:S(2)}) collective-permute-start(f32[96,1024]{1,0:T(8,128)S(1)} %add.67), channel_id=1, source_target_pairs={{0,8},{8,0},{16,24},{24,16},{1,9},{9,1},{17,25},{25,17},{2,10},{10... | collective-permute-start | bytes 1179656 | tf_op jit(solution)/shard_map/ppermute | solution.py:293
  115.7 10.6 %collective-permute-start.20 = (f32[864,128]{1,0:T(8,128)S(1)}, f32[864,128]{1,0:T(8,128)S(1)}, u32[]{:S(2)}, u32[]{:S(2)}) collective-permute-start(f32[864,128]{1,0:T(8,128)S(1)} %constant_dynamic-update-slice_fusion.2.refs_1_), channel_id=1, source_target_pairs={{0,16},{1,17},{10,26},{11,27},{20,4},{21,5},{30,14},{31,15}} | collective-permute-start | bytes 1327112 | tf_op jit(solution)/shard_map/ppermute | solution.py:419
  119.1 13.2 %collective-permute-start.22 = (f32[864,128]{1,0:T(8,128)S(1)}, f32[864,128]{1,0:T(8,128)S(1)}, u32[]{:S(2)}, u32[]{:S(2)}) collective-permute-start(f32[864,128]{1,0:T(8,128)S(1)} %constant_dynamic-update-slice_fusion.refs_0_), channel_id=1, source_target_pairs={{0,1},{1,0},{2,3},{3,2},{4,5},{5,4},{6,7},{7,6},{8,9},{9,8},{10,11... | collective-permute-start | bytes 1327112 | tf_op jit(solution)/shard_map/ppermute | solution.py:293
  119.5 19.3 %collective-permute-start.23 = (f32[864,128]{1,0:T(8,128)S(1)}, f32[864,128]{1,0:T(8,128)S(1)}, u32[]{:S(2)}, u32[]{:S(2)}) collective-permute-start(f32[864,128]{1,0:T(8,128)S(1)} %constant_dynamic-update-slice_fusion.2.refs_1_), channel_id=1, source_target_pairs={{0,1},{1,0},{2,3},{3,2},{4,5},{5,4},{6,7},{7,6},{8,9},{9,8},{10,11... | collective-permute-start | bytes 1327112 | tf_op jit(solution)/shard_map/ppermute | solution.py:293
  120.7 7.4 %collective-permute-start.19 = (f32[864,128]{1,0:T(8,128)S(1)}, f32[864,128]{1,0:T(8,128)S(1)}, u32[]{:S(2)}, u32[]{:S(2)}) collective-permute-start(f32[864,128]{1,0:T(8,128)S(1)} %broadcast_select_fusion.3), channel_id=1, source_target_pairs={{0,8},{16,24},{1,9},{17,25},{10,2},{26,18},{11,3},{27,19},{4,12},{... | collective-permute-start | bytes 1327112 | tf_op jit(solution)/shard_map/ppermute | solution.py:419
  126.4 2.7 %collective-permute-start.21 = (f32[864,128]{1,0:T(8,128)S(1)}, f32[864,128]{1,0:T(8,128)S(1)}, u32[]{:S(2)}, u32[]{:S(2)}) collective-permute-start(f32[864,128]{1,0:T(8,128)S(1)} %broadcast_select_fusion.2), channel_id=1, source_target_pairs={{0,8},{16,24},{1,9},{17,25},{10,2},{26,18},{11,3},{27,19},{4,12},{... | collective-permute-start | bytes 1327112 | tf_op jit(solution)/shard_map/ppermute | solution.py:419
